TPU v7x, 256 devices: a whole 4x4x8 slice. The times are simulated.
256 devices in a mesh: dp: 16 (over z, core), tx: 4 (over y), ty: 4 (over x).
Axes of the slice: x: 4, y: 4, z: 8, core: 2. Of those that a mesh axis runs over, the one named last changes fastest.
Arguments:
- hidden_in: bfloat16 [8192, 2048], P('dp', 'ty'), may hold values from -24 to 24
- norm_gain: bfloat16 [2048], replicated, may hold values from 0.099609375 to 1.8984375
- w_qkv: bfloat16 [2048, 3072], P('ty', 'tx'), may hold values from -16 to 16
- w_out: bfloat16 [2048, 2048], P('tx', 'ty'), may hold values from -0.125 to 0.125
- k_cache: bfloat16 [128, 8192, 512], P('dp', 'ty', 'tx'), may hold values from -3300 to 3300
- v_cache: bfloat16 [128, 8192, 512], P('dp', 'ty', 'tx'), may hold values from -6.5 to 6.5
- cache_lens: int32 [128], replicated, may hold values from 1 to 8192, 524288 in all
- home_slot: int32 [128], replicated, may hold values from 0 to 127, as said below
- parents: int32 [128, 64], replicated, may hold values from 0 to 6, as said below
- tree_sizes: int32 [128], P('dp'), may hold values from 32 to 64, as said below
- leaf_node: int32 [128], P('dp'), may hold values from 0 to 31
Outputs:
- layer_out: bfloat16 [8192, 2048], P(('dp', 'tx'), 'ty')
- accepted_kv: bfloat16 [128, 8, 2, 512], P('dp', None, None, 'tx')
Inputs may be any that keep to these rules, and one draw needn't show every extreme that they name: A permutation of the 128 cache slots; the slot lies in group home_slot[r] // 8 of dp. Of the 8 requests of one group, at most 1 have their slots in any one group, and 1 is reached. parents[r, 0] = 0 is the root; parents[r, t] = t - 1 for 0 < t < 8; every other node's parent is one of the nodes 0 to 6. Slots from tree_sizes[r] to 63 are padding; some request fills all 64. Positions from cache_lens[s] on in slot s are unused; some slot is full.
All inputs are finite; a program needn't handle non-finite values.
Results may differ from a plain program's by a relative error of at most 0.012.
Values may be sent and summed in bfloat16 or wider, within the bound.
A program may use at most 128 MiB of HBM per device.

v0:
```python
import functools

import jax
import jax.numpy as jnp
from jax import lax
from jax.experimental import pallas as pl
from jax.experimental.pallas import tpu as pltpu
from jax.sharding import PartitionSpec as P

D = 2048
HD = 64
GROUP = 4
ACC = 8


rope_base = 10000000.0
attn_mult = 0.015625
norm_eps = 1e-05
neg_fill = -1e30


def joined(value, axis, join):
    pieces = jax.tree.map(lambda part: lax.all_gather(part, axis), value)
    head = jax.tree.map(lambda part: part[0], pieces)
    tail = jax.tree.map(lambda part: part[1:], pieces)
    so_far, _ = lax.scan(lambda so_far, slab: (join(so_far, slab), None), head, tail)
    return so_far


def ancestry(parent_rows):
    node_count = parent_rows.shape[-1]
    node_ids = jnp.arange(node_count, dtype=jnp.int32)
    linked = (node_ids[None, :] == parent_rows[:, None]) | (node_ids[None, :] == node_ids[:, None])
    reachable = linked.astype(jnp.float32)
    for repeat in range(max(1, (node_count - 1).bit_length())):
        reachable = jnp.minimum(jnp.dot(reachable, reachable, precision=lax.Precision.HIGHEST), 1.0)
    return reachable


def rotated(values, positions):
    half_size = values.shape[-1] // 2
    frequency = rope_base ** (-2.0 * jnp.arange(half_size, dtype=jnp.float32) / values.shape[-1])
    angles = positions.astype(jnp.float32)[..., None] * frequency
    cosine = jnp.cos(angles)
    sine_part = jnp.sin(angles)
    front_half = values[..., :half_size]
    back_half = values[..., half_size:]
    return jnp.concatenate(
        [front_half * cosine - back_half * sine_part, back_half * cosine + front_half * sine_part],
        axis=-1,
    )


def combine_stats(first_stats, second_stats):
    top_first, sum_first, summed_first = first_stats
    top_second, sum_second, summed_second = second_stats
    top_both = jnp.maximum(top_first, top_second)
    scale_first = jnp.exp(top_first - top_both)
    scale_second = jnp.exp(top_second - top_both)
    return (
        top_both,
        sum_first * scale_first + sum_second * scale_second,
        summed_first * scale_first[..., None] + summed_second * scale_second[..., None],
    )


def packed(values, index):
    return jnp.take(values, index, axis=0, mode="fill", fill_value=0)


def routing(home_slot, group_count, local_reqs):
    dest_group = (home_slot // local_reqs).reshape(group_count, local_reqs)
    local_ids = jnp.arange(local_reqs, dtype=jnp.int32)
    earlier = local_ids[None, :] < local_ids[:, None]
    same_dest = dest_group[:, :, None] == dest_group[:, None, :]
    dest_rank = jnp.sum(same_dest & earlier[None], axis=2)
    return (dest_group, dest_rank)


def tree_part(queries, keys_new, values_new, ancestors):
    scores = attn_mult * jnp.einsum(
        "rtkgd,rukd->rtkgu", queries, keys_new, preferred_element_type=jnp.float32
    )
    valid_keys = (ancestors > 0.5)[:, :, None, None, :]
    masked = jnp.where(valid_keys, scores, neg_fill)
    top_score = jnp.max(masked, axis=-1)
    weights = jnp.where(valid_keys, jnp.exp(masked - top_score[..., None]), 0.0)
    summed = jnp.einsum(
        "rtkgu,rukd->rtkgd",
        weights.astype(jnp.bfloat16),
        values_new,
        preferred_element_type=jnp.float32,
    )
    return (top_score, jnp.sum(weights, axis=-1), summed)


def cache_kernel(lens_ref, start_ref, q_ref, k_ref, v_ref, top_ref, sum_ref, acc_ref):
    slot = pl.program_id(0)
    head_local = top_ref.shape[1]
    cache_local = k_ref.shape[1]
    limit = lens_ref[slot] - start_ref[0]
    valid = lax.broadcasted_iota(jnp.int32, (1, cache_local), 1) < limit
    keys = k_ref[0]
    values = v_ref[0]
    lane = lax.broadcasted_iota(jnp.int32, (1, head_local * HD), 1)
    queries = q_ref[0] * jnp.asarray(attn_mult, q_ref.dtype)
    any_valid = limit > 0
    result = None
    for head in range(head_local):
        mine = (lane >= head * HD) & (lane < (head + 1) * HD)
        own = jnp.where(mine, queries, jnp.zeros((), queries.dtype))
        scores = lax.dot_general(
            own, keys, (((1,), (1,)), ((), ())), preferred_element_type=jnp.float32
        )
        masked = jnp.where(valid, scores, neg_fill)
        top = jnp.max(masked, axis=1, keepdims=True)
        weights = jnp.exp(masked - top)
        summed = jnp.dot(weights.astype(jnp.bfloat16), values, preferred_element_type=jnp.float32)
        total = jnp.where(any_valid, jnp.sum(weights, axis=1, keepdims=True), 0.0)
        top_ref[0, head : head + 1, :] = jnp.broadcast_to(top, (top.shape[0], 128)).T[0:1, :]
        sum_ref[0, head : head + 1, :] = jnp.broadcast_to(total, (total.shape[0], 128)).T[0:1, :]
        result = summed if result is None else jnp.where(mine, summed, result)
    acc_ref[0] = jnp.where(any_valid, result, 0.0)


def cache_merged(slot_queries, k_cache, v_cache, home_lens):
    local_reqs, tree_slots, head_local = slot_queries.shape[:3]
    cache_local = k_cache.shape[1]
    width = head_local * HD
    rows = tree_slots * GROUP
    key_start = (lax.axis_index("ty") * cache_local).astype(jnp.int32).reshape(1)
    spread = slot_queries.transpose(0, 1, 3, 2, 4).reshape(local_reqs, rows, width)
    top, total, summed = pl.pallas_call(
        cache_kernel,
        grid_spec=pltpu.PrefetchScalarGridSpec(
            num_scalar_prefetch=2,
            grid=(local_reqs,),
            in_specs=[
                pl.BlockSpec((1, rows, width), lambda s, lens, start: (s, 0, 0)),
                pl.BlockSpec((1, cache_local, width), lambda s, lens, start: (s, 0, 0)),
                pl.BlockSpec((1, cache_local, width), lambda s, lens, start: (s, 0, 0)),
            ],
            out_specs=[
                pl.BlockSpec((1, head_local, rows), lambda s, lens, start: (s, 0, 0)),
                pl.BlockSpec((1, head_local, rows), lambda s, lens, start: (s, 0, 0)),
                pl.BlockSpec((1, rows, width), lambda s, lens, start: (s, 0, 0)),
            ],
        ),
        out_shape=[
            jax.ShapeDtypeStruct((local_reqs, head_local, rows), jnp.float32),
            jax.ShapeDtypeStruct((local_reqs, head_local, rows), jnp.float32),
            jax.ShapeDtypeStruct((local_reqs, rows, width), jnp.float32),
        ],
        cost_estimate=pl.CostEstimate(
            flops=4 * local_reqs * head_local * rows * cache_local * width,
            transcendentals=local_reqs * head_local * rows * cache_local,
            bytes_accessed=2 * k_cache.size * 2 + spread.size * 2 + local_reqs * rows * width * 4,
        ),
    )(home_lens, key_start, spread, k_cache, v_cache)
    top_all = ty_max(top)
    scale = jnp.exp(top - top_all)
    scale_lanes = jnp.repeat(scale.transpose(0, 2, 1), HD, axis=2)
    count = total.size
    joint = jnp.concatenate(
        [(summed * scale_lanes).reshape(-1, 128), (total * scale).reshape(count // 128, 128)],
        axis=0,
    )
    joint = axis_sum(joint, "ty", True, jnp.bfloat16, jnp.bfloat16, 2)[: joint.shape[0]]
    joint = joint.astype(jnp.float32)
    summed = joint[: summed.size // 128].reshape(summed.shape)
    total = joint[summed.size // 128 :].reshape(total.shape)
    return (top_all, total, summed)


def ty_max_kernel(x_ref, out_ref, held, send_sem, recv_sem):
    n = lax.axis_size("ty")
    me = lax.axis_index("ty")
    row = lax.axis_index("dp")
    col = lax.axis_index("tx")
    barrier = pltpu.get_barrier_semaphore()
    for step in range(1, n):
        peer = lax.rem(me + step, n)
        pl.semaphore_signal(
            barrier, inc=1, device_id=(row, col, peer), device_id_type=pl.DeviceIdType.MESH
        )
    pl.semaphore_wait(barrier, n - 1)
    copies = []
    for step in range(1, n):
        peer = lax.rem(me + step, n)
        copy = pltpu.make_async_remote_copy(
            src_ref=x_ref,
            dst_ref=held.at[step - 1],
            send_sem=send_sem.at[step - 1],
            recv_sem=recv_sem.at[step - 1],
            device_id=(row, col, peer),
            device_id_type=pl.DeviceIdType.MESH,
        )
        copy.start()
        copies.append(copy)
    for copy in copies:
        copy.wait()
    result = x_ref[...]
    for step in range(1, n):
        result = jnp.maximum(result, held[step - 1])
    out_ref[...] = result


def axis_sum_kernel(axis, gather, x_ref, out_ref, held, gathered, sems):
    n = lax.axis_size(axis)
    me = lax.axis_index(axis)
    chunk = held.shape[1]
    where = {name: lax.axis_index(name) for name in ("dp", "tx", "ty")}

    def device(peer):
        return tuple(peer if name == axis else where[name] for name in ("dp", "tx", "ty"))

    barrier = pltpu.get_barrier_semaphore()
    for step in range(1, n):
        pl.semaphore_signal(
            barrier, inc=1, device_id=device(lax.rem(me + step, n)), device_id_type=pl.DeviceIdType.MESH
        )
    pl.semaphore_wait(barrier, n - 1)
    copies = []
    for step in range(1, n):
        peer = lax.rem(me + step, n)
        copy = pltpu.make_async_remote_copy(
            src_ref=x_ref.at[pl.ds(pl.multiple_of(peer * chunk, 16), chunk)],
            dst_ref=held.at[step - 1],
            send_sem=sems.at[0, step - 1],
            recv_sem=sems.at[1, step - 1],
            device_id=device(peer),
            device_id_type=pl.DeviceIdType.MESH,
        )
        copy.start()
        copies.append(copy)
    for copy in copies:
        copy.wait()
    own = pl.ds(pl.multiple_of(me * chunk, 16), chunk)
    total = x_ref[own].astype(jnp.float32)
    for step in range(1, n):
        total = total + held[step - 1].astype(jnp.float32)
    if not gather:
        out_ref[...] = total.astype(out_ref.dtype)
        return
    out_ref[own] = total.astype(out_ref.dtype)
    copies = []
    for step in range(1, n):
        peer = lax.rem(me + step, n)
        copy = pltpu.make_async_remote_copy(
            src_ref=out_ref.at[own],
            dst_ref=gathered.at[step - 1],
            send_sem=sems.at[2, step - 1],
            recv_sem=sems.at[3, step - 1],
            device_id=device(peer),
            device_id_type=pl.DeviceIdType.MESH,
        )
        copy.start()
        copies.append(copy)
    for copy in copies:
        copy.wait()
    for step in range(1, n):
        source = lax.rem(me - step + n, n)
        out_ref[pl.ds(pl.multiple_of(source * chunk, 16), chunk)] = gathered[step - 1]


def axis_sum(values, axis, gather, send_type, out_type, collective_id):
    n = lax.axis_size(axis)
    flat = values.reshape(-1, 128).astype(send_type)
    rows = flat.shape[0]
    padded = -(-rows // (16 * n)) * 16 * n
    flat = jnp.pad(flat, ((0, padded - rows), (0, 0)))
    chunk = padded // n
    out = pl.pallas_call(
        functools.partial(axis_sum_kernel, axis, gather),
        out_shape=jax.ShapeDtypeStruct((padded if gather else chunk, 128), out_type),
        in_specs=[pl.BlockSpec(memory_space=pltpu.VMEM)],
        out_specs=pl.BlockSpec(memory_space=pltpu.VMEM),
        scratch_shapes=[
            pltpu.VMEM((n - 1, chunk, 128), send_type),
            pltpu.VMEM((n - 1, chunk, 128), out_type),
            pltpu.SemaphoreType.DMA((4, n - 1)),
        ],
        compiler_params=pltpu.CompilerParams(collective_id=collective_id, has_side_effects=True),
    )(flat)
    return out


def dp_exchange_kernel(x_ref, out_ref, held, sems):
    n = lax.axis_size("dp")
    me = lax.axis_index("dp")
    col = lax.axis_index("tx")
    row = lax.axis_index("ty")
    barrier = pltpu.get_barrier_semaphore()
    for step in range(1, n):
        pl.semaphore_signal(
            barrier, inc=1, device_id=(lax.rem(me + step, n), col, row), device_id_type=pl.DeviceIdType.MESH
        )
    pl.semaphore_wait(barrier, n - 1)
    copies = []
    for step in range(1, n):
        peer = lax.rem(me + step, n)
        copy = pltpu.make_async_remote_copy(
            src_ref=x_ref.at[peer],
            dst_ref=held.at[step - 1],
            send_sem=sems.at[0, step - 1],
            recv_sem=sems.at[1, step - 1],
            device_id=(peer, col, row),
            device_id_type=pl.DeviceIdType.MESH,
        )
        copy.start()
        copies.append(copy)
    out_ref[me] = x_ref[me]
    for copy in copies:
        copy.wait()
    for step in range(1, n):
        out_ref[lax.rem(me - step + n, n)] = held[step - 1]


def dp_exchange(blocks, collective_id):
    n = lax.axis_size("dp")
    shape = blocks.shape
    tiles = blocks.reshape(n, -1, 128)
    out = pl.pallas_call(
        dp_exchange_kernel,
        out_shape=jax.ShapeDtypeStruct(tiles.shape, tiles.dtype),
        in_specs=[pl.BlockSpec(memory_space=pltpu.VMEM)],
        out_specs=pl.BlockSpec(memory_space=pltpu.VMEM),
        scratch_shapes=[
            pltpu.VMEM((n - 1,) + tiles.shape[1:], tiles.dtype),
            pltpu.SemaphoreType.DMA((2, n - 1)),
        ],
        compiler_params=pltpu.CompilerParams(collective_id=collective_id, has_side_effects=True),
    )(tiles)
    return out.reshape(shape)


def axis_gather_kernel(axis, x_ref, out_ref, gathered, sems):
    n = lax.axis_size(axis)
    me = lax.axis_index(axis)
    chunk = x_ref.shape[0]
    where = {name: lax.axis_index(name) for name in ("dp", "tx", "ty")}

    def device(peer):
        return tuple(peer if name == axis else where[name] for name in ("dp", "tx", "ty"))

    barrier = pltpu.get_barrier_semaphore()
    for step in range(1, n):
        pl.semaphore_signal(
            barrier, inc=1, device_id=device(lax.rem(me + step, n)), device_id_type=pl.DeviceIdType.MESH
        )
    pl.semaphore_wait(barrier, n - 1)
    copies = []
    for step in range(1, n):
        peer = lax.rem(me + step, n)
        copy = pltpu.make_async_remote_copy(
            src_ref=x_ref,
            dst_ref=gathered.at[step - 1],
            send_sem=sems.at[0, step - 1],
            recv_sem=sems.at[1, step - 1],
            device_id=device(peer),
            device_id_type=pl.DeviceIdType.MESH,
        )
        copy.start()
        copies.append(copy)
    out_ref[pl.ds(pl.multiple_of(me * chunk, 16), chunk)] = x_ref[...]
    for copy in copies:
        copy.wait()
    for step in range(1, n):
        source = lax.rem(me - step + n, n)
        out_ref[pl.ds(pl.multiple_of(source * chunk, 16), chunk)] = gathered[step - 1]


def axis_gather(values, axis, collective_id):
    n = lax.axis_size(axis)
    flat = values.reshape(-1, 128)
    chunk = flat.shape[0]
    out = pl.pallas_call(
        functools.partial(axis_gather_kernel, axis),
        out_shape=jax.ShapeDtypeStruct((n * chunk, 128), flat.dtype),
        in_specs=[pl.BlockSpec(memory_space=pltpu.VMEM)],
        out_specs=pl.BlockSpec(memory_space=pltpu.VMEM),
        scratch_shapes=[
            pltpu.VMEM((n - 1, chunk, 128), flat.dtype),
            pltpu.SemaphoreType.DMA((2, n - 1)),
        ],
        compiler_params=pltpu.CompilerParams(collective_id=collective_id, has_side_effects=True),
    )(flat)
    return out.reshape((n * values.shape[0],) + values.shape[1:])


def ty_max(values):
    n = lax.axis_size("ty")
    flat = values.reshape(-1, 128)
    out = pl.pallas_call(
        ty_max_kernel,
        out_shape=jax.ShapeDtypeStruct(flat.shape, flat.dtype),
        in_specs=[pl.BlockSpec(memory_space=pltpu.VMEM)],
        out_specs=pl.BlockSpec(memory_space=pltpu.VMEM),
        scratch_shapes=[
            pltpu.VMEM((n - 1,) + flat.shape, flat.dtype),
            pltpu.SemaphoreType.DMA((n - 1,)),
            pltpu.SemaphoreType.DMA((n - 1,)),
        ],
        compiler_params=pltpu.CompilerParams(collective_id=0, has_side_effects=True),
    )(flat)
    return out.reshape(values.shape)


def shards(
    hidden_in,
    norm_gain,
    w_qkv,
    w_out,
    k_cache,
    v_cache,
    cache_lens,
    home_slot,
    parents,
    tree_sizes,
    leaf_node,
):
    group_count = lax.axis_size("dp")
    group_index = lax.axis_index("dp")
    local_reqs = k_cache.shape[0]
    tree_slots = parents.shape[1]
    capacity = (local_reqs + group_count - 1) // group_count
    head_local = k_cache.shape[2] // HD
    row_count = hidden_in.shape[0]
    float_in = hidden_in.astype(jnp.float32)
    feature_local = hidden_in.shape[1]
    gain_part = lax.dynamic_slice_in_dim(
        norm_gain, lax.axis_index("ty") * feature_local, feature_local
    )
    scaled = (float_in * gain_part.astype(jnp.float32)).astype(jnp.bfloat16)
    partial_proj = jnp.dot(scaled, w_qkv, preferred_element_type=jnp.float32)
    partial_square = jnp.sum(float_in * float_in, axis=1)
    proj_cols = partial_proj.shape[1]
    n_ty = lax.axis_size("ty")
    chunk_rows = row_count // n_ty
    reqs_mine = local_reqs // n_ty
    square_block = jnp.pad(
        partial_square.reshape(n_ty, 1, chunk_rows),
        ((0, 0), (0, 7), (0, proj_cols - chunk_rows)),
    )
    joint = jnp.concatenate(
        [partial_proj.reshape(n_ty, chunk_rows, proj_cols), square_block], axis=1
    )
    mine = axis_sum(joint, "ty", False, jnp.float32, jnp.float32, 1).reshape(-1, proj_cols)
    square_sum = mine[chunk_rows, :chunk_rows]
    rms_inverse = lax.rsqrt(square_sum / D + norm_eps)
    projected = (mine[:chunk_rows] * rms_inverse[:, None]).reshape(
        reqs_mine, tree_slots, head_local, GROUP + 2, HD
    )
    first_request = group_index * local_reqs
    local_ids = jnp.arange(local_reqs, dtype=jnp.int32)
    request_ids = jnp.arange(home_slot.shape[0], dtype=jnp.int32)
    my_parents = lax.dynamic_slice_in_dim(parents, first_request, local_reqs, 0)
    my_slots = lax.dynamic_slice_in_dim(home_slot, first_request, local_reqs, 0)
    ancestors = jax.vmap(ancestry)(my_parents)
    node_depth = jnp.sum(ancestors > 0.5, axis=2) - 1
    slot_match = my_slots[:, None] == request_ids[None, :]
    my_lens = jnp.sum(jnp.where(slot_match, cache_lens[None, :], 0), axis=1)
    positions = my_lens[:, None] + node_depth
    positions_mine = lax.dynamic_slice_in_dim(
        positions, lax.axis_index("ty") * reqs_mine, reqs_mine, 0
    )
    queries_mine = rotated(
        projected[:, :, :, :GROUP, :], positions_mine[:, :, None, None]
    ).astype(jnp.bfloat16)
    keys_mine = rotated(projected[:, :, :, GROUP, :], positions_mine[:, :, None]).astype(
        jnp.bfloat16
    )
    values_mine = projected[:, :, :, GROUP + 1, :].astype(jnp.bfloat16)
    piece = jnp.concatenate(
        [
            queries_mine.reshape(chunk_rows, -1),
            keys_mine.reshape(chunk_rows, -1),
            values_mine.reshape(chunk_rows, -1),
        ],
        axis=1,
    )
    everything = axis_gather(piece, "ty", 6)
    query_cols = head_local * GROUP * HD
    queries = everything[:, :query_cols].reshape(local_reqs, tree_slots, head_local, GROUP, HD)
    keys_new = everything[:, query_cols : query_cols + head_local * HD].reshape(
        local_reqs, tree_slots, head_local, HD
    )
    values_new = everything[:, query_cols + head_local * HD :].reshape(
        local_reqs, tree_slots, head_local, HD
    )
    dest_group, dest_rank = routing(home_slot, group_count, local_reqs)
    send_pos = lax.dynamic_index_in_dim(
        dest_group, group_index, 0, keepdims=False
    ) * capacity + lax.dynamic_index_in_dim(dest_rank, group_index, 0, keepdims=False)
    buffer_ids = jnp.arange(group_count * capacity, dtype=jnp.int32)
    send_hit = send_pos[None, :] == buffer_ids[:, None]
    send_index = jnp.where(
        jnp.any(send_hit, axis=1),
        jnp.sum(jnp.where(send_hit, local_ids[None, :], 0), axis=1),
        local_reqs,
    )
    target_slots = first_request + local_ids
    owner_match = home_slot[None, :] == target_slots[:, None]
    owner_request = jnp.sum(jnp.where(owner_match, request_ids[None, :], 0), axis=1)
    owner_rank = jnp.sum(jnp.where(owner_match, dest_rank.reshape(-1)[None, :], 0), axis=1)
    recv_index = owner_request // local_reqs * capacity + owner_rank
    back_hit = recv_index[None, :] == buffer_ids[:, None]
    back_index = jnp.where(
        jnp.any(back_hit, axis=1),
        jnp.sum(jnp.where(back_hit, local_ids[None, :], 0), axis=1),
        local_reqs,
    )
    home_lens = lax.dynamic_slice_in_dim(cache_lens, first_request, local_reqs, 0)
    arrived = dp_exchange(packed(queries.reshape(local_reqs, -1), send_index), 4)
    slot_queries = packed(arrived, recv_index).reshape(queries.shape)
    top_score, weight_sum, summed = cache_merged(slot_queries, k_cache, v_cache, home_lens)
    normalized = summed / jnp.repeat(weight_sum.transpose(0, 2, 1), HD, axis=2)
    log_total = top_score + jnp.log(weight_sum)
    value_width = normalized.size // local_reqs
    log_flat = log_total.reshape(local_reqs, -1)
    log_high = lax.reduce_precision(log_flat, exponent_bits=8, mantissa_bits=7)
    log_rest = log_flat - log_high
    log_mid = lax.reduce_precision(log_rest, exponent_bits=8, mantissa_bits=7)
    log_low = log_rest - log_mid
    payload = jnp.concatenate(
        [normalized.reshape(local_reqs, -1), log_high, log_mid, log_low], axis=1
    ).astype(jnp.bfloat16)
    back = lax.all_to_all(
        packed(payload, back_index), "dp", split_axis=0, concat_axis=0, tiled=True
    )
    back = packed(back, send_pos).astype(jnp.float32)
    log_width = log_flat.shape[1]
    cache_values = (
        back[:, :value_width]
        .reshape(local_reqs, tree_slots, GROUP, head_local, HD)
        .transpose(0, 1, 3, 2, 4)
    )
    cache_top = (
        (
            back[:, value_width : value_width + log_width]
            + back[:, value_width + log_width : value_width + 2 * log_width]
            + back[:, value_width + 2 * log_width :]
        )
        .reshape(local_reqs, head_local, tree_slots, GROUP)
        .transpose(0, 2, 1, 3)
    )
    tree_stats = tree_part(queries, keys_new, values_new, ancestors)
    top_all, sum_all, summed_all = combine_stats(
        (cache_top, jnp.ones_like(cache_top), cache_values), tree_stats
    )
    attention = (summed_all / sum_all[..., None]).astype(jnp.bfloat16)
    attention_rows = attention.reshape(row_count, -1)
    rows_mine = row_count // lax.axis_size("tx")
    mixed_sum = axis_sum(
        jnp.dot(attention_rows, w_out, preferred_element_type=jnp.float32),
        "tx",
        False,
        jnp.bfloat16,
        jnp.float32,
        3,
    ).reshape(row_count // lax.axis_size("tx"), -1)
    row_start = lax.axis_index("tx") * rows_mine
    residual = lax.dynamic_slice_in_dim(float_in, row_start, rows_mine, 0)
    row_ids = row_start + jnp.arange(rows_mine, dtype=jnp.int32)
    request_of = row_ids // tree_slots
    slot_of = row_ids % tree_slots
    size_of = jnp.sum(
        jnp.where(request_of[:, None] == local_ids[None, :], tree_sizes[None, :], 0), axis=1
    )
    layer_out = jnp.where((slot_of < size_of)[:, None], residual + mixed_sum, 0.0).astype(
        jnp.bfloat16
    )
    node_ids = jnp.arange(tree_slots, dtype=jnp.int32)
    leaf_hit = (leaf_node[:, None] == node_ids[None, :]).astype(jnp.float32)
    path_nodes = jnp.einsum("rt,rtu->ru", leaf_hit, ancestors)
    depth_hit = node_depth[:, None, :] == jnp.arange(ACC, dtype=jnp.int32)[None, :, None]
    chooser = jnp.where(depth_hit, path_nodes[:, None, :], 0.0).astype(jnp.bfloat16)
    stacked = jnp.stack(
        [
            keys_new.reshape(local_reqs, tree_slots, -1),
            values_new.reshape(local_reqs, tree_slots, -1),
        ],
        axis=2,
    )
    accepted_kv = jnp.einsum(
        "rsu,ruwc->rswc", chooser, stacked, preferred_element_type=jnp.float32
    ).astype(jnp.bfloat16)
    return (layer_out, accepted_kv)


def solution(mesh):
    return jax.shard_map(
        shards,
        mesh=mesh,
        in_specs=(
            P("dp", "ty"),
            P(),
            P("ty", "tx"),
            P("tx", "ty"),
            P("dp", "ty", "tx"),
            P("dp", "ty", "tx"),
            P(),
            P(),
            P(),
            P("dp"),
            P("dp"),
        ),
        out_specs=(P(("dp", "tx"), "ty"), P("dp", None, None, "tx")),
        check_vma=False,
    )
```

profile of v0, /device:TPU:1, one launch (start us, length us, event | category | flops | bytes accessed | tf_op | source)
XLA Modules:
  0.0 242.3 jit_solution(16906772846504362634)
XLA Ops:
  0.7 1.3 multiply_reduce_fusion
  2.7 1.6 fusion.18
  4.5 1.3 reshape.463.x_ref
  5.8 24.3 %shard_map.122 = f32[816,128]{1,0:T(8,128)} custom-call(f32[3264,128]{1,0:T(8,128)} %reshape.463.x_ref), custom_call_target="tpu_custom_call" | custom-call | tf_op jit(solution)/shard_map/pallas_call | solution.py:273
  41.9 15.0 %shard_map.123 = bf16[3072,128]{1,0:T(8,128)(2,1)} custom-call(bf16[768,128]{1,0:T(8,128)(2,1)} %reshape.465.x_ref), custom_call_target="tpu_custom_call" | custom-call | tf_op jit(solution)/shard_map/pallas_call | solution.py:377
  57.0 2.0 reshape.466
  59.3 1.2 gather_fusion
  61.8 35.1 %shard_map.124 = bf16[16,256,128]{2,1,0:T(8,128)(2,1)} custom-call(bf16[16,256,128]{2,1,0:T(8,128)(2,1)} %bitcast_select_fusion.2.x_ref), custom_call_target="tpu_custom_call" | custom-call | tf_op jit(solution)/shard_map/pallas_call | solution.py:323
  96.9 1.9 copy.182
  102.0 1.3 reshape.468.q_ref
  103.3 18.0 %shard_map.125 = (f32[8,2,256]{2,1,0:T(2,128)}, f32[8,2,256]{2,1,0:T(2,128)}, f32[8,256,128]{2,1,0:T(8,128)}) custom-call(s32[8]{0:T(128)} %dynamic_slice.28.lens_ref, s32[1]{0:T(128)} %bitcast.start_ref, bf16[8,256,128]{2,1,0:T(8,128)(2,1)} %reshape.468.q_ref, bf16[8,2048,128]{2,1,0:T(8,128)(2,1)} %k_ref.1, bf16[8,2048,128]{2,1,0:T(8,128)(2,1)} %v_ref.1), custom_call_target="tpu_custom_call" | custom-call | flops 4294967296 | bytes 9961472 | tf_op jit(solution)/shard_map/pallas_call | solution.py:133
  121.3 1.3 reshape.469.x_ref
  122.7 5.8 %shard_map.126 = f32[32,128]{1,0:T(8,128)} custom-call(f32[32,128]{1,0:T(8,128)} %reshape.469.x_ref), custom_call_target="tpu_custom_call" | custom-call | tf_op jit(solution)/shard_map/pallas_call | solution.py:394
  130.4 1.3 multiply_convert_fusion
  132.6 17.9 %shard_map.127 = bf16[2112,128]{1,0:T(8,128)(2,1)} custom-call(bf16[2112,128]{1,0:T(8,128)(2,1)} %fusion.17.x_ref), custom_call_target="tpu_custom_call" | custom-call | tf_op jit(solution)/shard_map/pallas_call | solution.py:273
  153.2 1.4 copy.128
  154.7 4.0 %broadcast_in_dim.217 = f32[8,256,2,64]{3,2,1,0:T(2,128)S(1)} broadcast(f32[8,256,2]{2,1,0:T(8,128)} %copy.128), dimensions={0,1,2} | broadcast | bytes 1064960 | tf_op jit(solution)/shard_map/broadcast_in_dim | solution.py:517
  158.6 3.0 %reshape.476 = f32[8,32768]{1,0:T(8,128)} reshape(f32[8,256,2,64]{3,2,1,0:T(2,128)S(1)} %broadcast_in_dim.217) | data formatting | bytes 2097152 | tf_op jit(solution)/shard_map/reshape | solution.py:517
  161.6 1.5 reshape.474
  163.2 1.3 add.252
  165.4 1.3 gather_fusion.2
  168.4 2.7 %reduce.11 = bf16[16,34304]{1,0:T(8,128)(2,1)S(1)} reduce(bf16[16,1,34304]{2,0,1:T(8,128)(2,1)} %bitcast_select_fusion.1, bf16[]{:T(256)} %broadcast.559), dimensions={1}, to_apply=%copy.129.reduce_sub_computation | reduce | bytes 2195458 | tf_op jit(solution)/shard_map/jit(_take)/select_n | solution.py:68
  172.3 8.0 %all-to-all-start = ((bf16[16,2,17152]{2,1,0:T(2,128)(2,1)}), bf16[16,2,17152]{2,1,0:T(2,128)(2,1)}, u32[]{:S(2)}, u32[]{:S(2)}) async-start(bf16[16,2,17152]{2,1,0:T(2,128)(2,1)} %reshape.532), calls=%async_computation | async-start | bytes 2195456 | tf_op jit(solution)/shard_map/all_to_all | solution.py:528
  184.8 1.2 fusion.3
  186.0 1.3 copy-done.2
  188.1 21.2 %all-to-all-done = bf16[16,2,17152]{2,1,0:T(2,128)(2,1)} async-done(((bf16[16,2,17152]{2,1,0:T(2,128)(2,1)}), bf16[16,2,17152]{2,1,0:T(2,128)(2,1)}, u32[]{:S(2)}, u32[]{:S(2)}) %all-to-all-start) | async-done | bytes 1097760 | tf_op jit(solution)/shard_map/all_to_all | solution.py:528
  209.3 4.2 %reshape.533 = bf16[16,1,34304]{2,1,0:T(2,128)(2,1)S(1)} reshape(bf16[16,2,17152]{2,1,0:T(2,128)(2,1)} %all-to-all-done) | data formatting | bytes 2195456
  215.1 2.9 %reshape.477 = f32[8,64,4,2,64]{4,3,2,1,0:T(2,128)} reshape(f32[8,32768]{1,0:T(8,128)S(1)} %slice.98) | data formatting | bytes 2097152 | tf_op jit(solution)/shard_map/reshape | solution.py:535
  218.0 4.3 %copy.130 = f32[8,64,4,2,64]{1,4,2,3,0:T(8,128)} copy(f32[8,64,4,2,64]{4,3,2,1,0:T(2,128)} %reshape.477) | data formatting | bytes 2097152 | tf_op jit(solution)/shard_map/reshape | solution.py:535
  222.3 2.5 %fusion.2 = bf16[8,64,2,4,64]{1,4,3,2,0:T(8,128)(2,1)S(1)} fusion(f32[8,64,4,2,64]{1,4,2,3,0:T(8,128)} %copy.130, f32[8,2,64,64,4]{3,2,4,1,0:T(8,128)S(1)} %copy-done.3, f32[8,64,2,4]{1,3,2,0:T(4,128)S(1)} %get-tuple-element.22, f32[8,64,2,4]{1,3,2,0:T(4,128)S(1)} %get-tuple-element.23, f32[8,64,2,4]{1,3,2,0:T(4,128)S(1)} %get-tuple-element.46, ...), kind=kOutput, calls=%fused_computation.7 | convolution fusion | flops 36175872 | bytes 2850816 | tf_op jit(solution)/shard_map/rtkgu,rukd->rtkgd/dot_general | solution.py:88
  227.7 11.8 %shard_map.128 = f32[512,128]{1,0:T(8,128)} custom-call(bf16[2048,128]{1,0:T(8,128)(2,1)} %convert_element_type.84.x_ref), custom_call_target="tpu_custom_call" | custom-call | tf_op jit(solution)/shard_map/pallas_call | solution.py:273
  240.5 1.7 select_convert_fusion.1
  (151 shorter events, 37.0 us)
Async XLA Ops:
  0.6 2.1 copy-start
  30.1 1.2 slice-start
  31.3 1.2 copy-start.12
  31.5 3.3 %copy-start.8 = (s32[128,64]{0,1:T(8,128)S(1)}, s32[128,64]{0,1:T(8,128)}, u32[]{:S(2)}) copy-start(s32[128,64]{0,1:T(8,128)} %param.19) | copy-start | bytes 98308
  33.5 3.4 %copy-start.13 = (s32[8]{0:T(128)}, s32[8]{0:T(128)S(1)}, u32[]{:S(2)}) copy-start(s32[8]{0:T(128)S(1)} %add_reduce_fusion) | copy-start | bytes 100
  35.7 1.9 copy-start.16
  131.7 19.8 %copy-start.7 = (f32[32,128]{1,0:T(8,128)S(1)}, f32[32,128]{1,0:T(8,128)}, u32[]{:S(2)}) copy-start(f32[32,128]{1,0:T(8,128)} %shard_map.126) | copy-start | bytes 49156
  161.6 3.6 %copy-start.11 = (s32[16]{0:T(128)S(1)}, s32[16]{0:T(128)}, u32[]{:S(2)}) copy-start(s32[16]{0:T(128)} %get-tuple-element.51) | copy-start | bytes 196
  161.6 3.6 %copy-start.5 = (f32[8,32768]{1,0:T(8,128)S(1)}, f32[8,32768]{1,0:T(8,128)}, u32[]{:S(2)}) copy-start(f32[8,32768]{1,0:T(8,128)} %reshape.476) | copy-start | bytes 3145732
  165.4 1.3 copy-start.10
  172.3 8.1 %copy-start.17 = (s32[8]{0:T(128)S(1)}, s32[8]{0:T(128)}, u32[]{:S(2)}) copy-start(s32[8]{0:T(128)} %param.21) | copy-start | bytes 100
  172.3 8.8 %copy-start.4 = (bf16[512,512]{1,0:T(8,128)(2,1)S(1)}, bf16[512,512]{1,0:T(8,128)(2,1)}, u32[]{:S(2)}) copy-start(bf16[512,512]{1,0:T(8,128)(2,1)} %param.11) | copy-start | bytes 1572868
  172.3 37.1 %all-to-all-start = ((bf16[16,2,17152]{2,1,0:T(2,128)(2,1)}), bf16[16,2,17152]{2,1,0:T(2,128)(2,1)}, u32[]{:S(2)}, u32[]{:S(2)}) async-start(bf16[16,2,17152]{2,1,0:T(2,128)(2,1)} %reshape.532), calls=%async_computation | async-start | bytes 2195456 | tf_op jit(solution)/shard_map/all_to_all | solution.py:528
  181.0 2.8 %copy-start.9 = (s32[8,64]{1,0:T(8,128)S(1)}, s32[8,64]{1,0:T(8,128)}, u32[]{:S(2)}) copy-start(s32[8,64]{1,0:T(8,128)} %get-tuple-element.40) | copy-start | bytes 6148
  181.0 3.6 %copy-start.14 = (s32[8]{0:T(128)S(1)}, s32[8]{0:T(128)}, u32[]{:S(2)}) copy-start(s32[8]{0:T(128)} %copy-done.13) | copy-start | bytes 100
  181.1 3.6 %copy-start.18 = (s32[8]{0:T(128)S(1)}, s32[8]{0:T(128)}, u32[]{:S(2)}) copy-start(s32[8]{0:T(128)} %param.20) | copy-start | bytes 100
  186.0 1.4 copy-start.2
  218.0 4.3 %copy-start.3 = (f32[8,2,64,64,4]{3,2,4,1,0:T(8,128)S(1)}, f32[8,2,64,64,4]{3,2,4,1,0:T(8,128)}, u32[]{:S(2)}) copy-start(f32[8,2,64,64,4]{3,2,4,1,0:T(8,128)} %copy-done.2) | copy-start | bytes 3145732
  218.0 4.3 %copy-start.6 = (bf16[8,64,2,64]{1,0,3,2:T(8,128)(2,1)S(1)}, bf16[8,64,2,64]{1,0,3,2:T(8,128)(2,1)}, u32[]{:S(2)}) copy-start(bf16[8,64,2,64]{1,0,3,2:T(8,128)(2,1)} %reshape.481) | copy-start | bytes 393220
  224.8 1.3 copy-start.15
  226.1 16.1 %copy-start.1 = (bf16[512,768]{1,0:T(8,128)(2,1)S(1)}, bf16[512,768]{1,0:T(8,128)(2,1)}, u32[]{:S(2)}) copy-start(bf16[512,768]{1,0:T(8,128)(2,1)} %param.13) | copy-start | bytes 2359300
where the time goes:
time: 244 us; the launch traced here: 242 us
  Pallas kernels  128 us (52%)
  local copies, waits for them, and re-layouts  52.6 us (22%)
  other arithmetic  22.7 us (9%)
  waiting for transfers between devices  21.2 us (9%)
  matrix products  8.31 us (3%)
  starting transfers between devices  8.05 us (3%)
    pallas_call x3, Pallas kernels, axis_sum(): pl.pallas_call(functools.partial(axis_sum_kernel, axis, gather), out_shap...  54 us
    pallas_call x1, Pallas kernels, dp_exchange(): pl.pallas_call(dp_exchange_kernel, out_shape=jax.ShapeDtypeStruct(tiles.s...  35.1 us
    all_to_all x1, waiting for transfers between devices, shards(): lax.all_to_all(packed(payload, back_index), 'dp', split_axis=0, concat_ax...  21.2 us
    pallas_call x1, Pallas kernels, cache_merged(): pl.pallas_call(cache_kernel, grid_spec=pltpu.PrefetchScalarGridSpec(num_s...  18 us
    pallas_call x1, Pallas kernels, axis_gather(): pl.pallas_call(functools.partial(axis_gather_kernel, axis), out_shape=jax...  15 us
    unnamed x46, local copies, waits for them, and re-layouts  9.9 us
    all_to_all x1, starting transfers between devices, shards(): lax.all_to_all(packed(payload, back_index), 'dp', split_axis=0, concat_ax...  8.05 us
    reshape x2, local copies, waits for them, and re-layouts, shards(): cache_values = back[:, :value_width].reshape(local_reqs, tree_slots, GROU...  7.16 us
  transfers between devices with their start and end apart: 1, of which 1 were waited for; matrix products, arithmetic and copies ran while one was open for 3% of the time, Pallas kernels for 0%

commit v1 on v0

--- a/solution.py
+++ b/solution.py
@@ -166,9 +166,8 @@
         axis=0,
     )
     joint = axis_sum(joint, "ty", True, jnp.bfloat16, jnp.bfloat16, 2)[: joint.shape[0]]
-    joint = joint.astype(jnp.float32)
-    summed = joint[: summed.size // 128].reshape(summed.shape)
-    total = joint[summed.size // 128 :].reshape(total.shape)
+    summed = joint[: summed.size // 128].reshape(summed.shape[0], -1)
+    total = joint[summed.size // 128 :].reshape(total.shape[0], -1)
     return (top_all, total, summed)
 
 
@@ -514,17 +513,23 @@
     arrived = dp_exchange(packed(queries.reshape(local_reqs, -1), send_index), 4)
     slot_queries = packed(arrived, recv_index).reshape(queries.shape)
     top_score, weight_sum, summed = cache_merged(slot_queries, k_cache, v_cache, home_lens)
-    normalized = summed / jnp.repeat(weight_sum.transpose(0, 2, 1), HD, axis=2)
-    log_total = top_score + jnp.log(weight_sum)
-    value_width = normalized.size // local_reqs
-    log_flat = log_total.reshape(local_reqs, -1)
+    value_width = summed.shape[1]
+    sum_width = weight_sum.shape[1]
+    log_flat = top_score.reshape(local_reqs, -1)
     log_high = lax.reduce_precision(log_flat, exponent_bits=8, mantissa_bits=7)
     log_rest = log_flat - log_high
     log_mid = lax.reduce_precision(log_rest, exponent_bits=8, mantissa_bits=7)
     log_low = log_rest - log_mid
     payload = jnp.concatenate(
-        [normalized.reshape(local_reqs, -1), log_high, log_mid, log_low], axis=1
-    ).astype(jnp.bfloat16)
+        [
+            summed,
+            weight_sum,
+            log_high.astype(jnp.bfloat16),
+            log_mid.astype(jnp.bfloat16),
+            log_low.astype(jnp.bfloat16),
+        ],
+        axis=1,
+    )
     back = lax.all_to_all(
         packed(payload, back_index), "dp", split_axis=0, concat_axis=0, tiled=True
     )
@@ -535,18 +540,24 @@
         .reshape(local_reqs, tree_slots, GROUP, head_local, HD)
         .transpose(0, 1, 3, 2, 4)
     )
+    cache_sum = (
+        back[:, value_width : value_width + sum_width]
+        .reshape(local_reqs, head_local, tree_slots, GROUP)
+        .transpose(0, 2, 1, 3)
+    )
+    logs = value_width + sum_width
     cache_top = (
         (
-            back[:, value_width : value_width + log_width]
-            + back[:, value_width + log_width : value_width + 2 * log_width]
-            + back[:, value_width + 2 * log_width :]
+            back[:, logs : logs + log_width]
+            + back[:, logs + log_width : logs + 2 * log_width]
+            + back[:, logs + 2 * log_width :]
         )
         .reshape(local_reqs, head_local, tree_slots, GROUP)
         .transpose(0, 2, 1, 3)
     )
     tree_stats = tree_part(queries, keys_new, values_new, ancestors)
     top_all, sum_all, summed_all = combine_stats(
-        (cache_top, jnp.ones_like(cache_top), cache_values), tree_stats
+        (cache_top, cache_sum, cache_values), tree_stats
     )
     attention = (summed_all / sum_all[..., None]).astype(jnp.bfloat16)
     attention_rows = attention.reshape(row_count, -1)

time: 244 us -> 233 us (0.955)
  waiting for transfers between devices: 21.2 us -> 14.6 us
  other arithmetic: 22.7 us -> 19.2 us
  local copies, waits for them, and re-layouts: 52.6 us -> 50.1 us
  matrix products: 8.31 us -> 10.8 us
    all_to_all x1, waiting for transfers between devices: 21.2 us -> 14.6 us  [shards(): lax.all_to_all(packed(payload, back_index), 'dp', split_axis=0, concat_ax...]
    reshape x4, local copies, waits for them, and re-layouts: 4.64 us -> 0.47 us  [the longest x1 0.23 us: cache_merged(): summed = joint[:summed.size // 128].reshape(summed.shape[0], -1)]
    broadcast_in_dim x1 -> x0, local copies, waits for them, and re-layouts: 3.97 us -> none  [shards(): normalized = summed / jnp.repeat(weight_sum.transpose(0, 2, 1), HD, axis=2)]
    unnamed x46 -> x44, local copies, waits for them, and re-layouts: 9.9 us -> 13.6 us
  transfers between devices with their start and end apart: 1 -> 1, of which waited for: 1 -> 1; matrix products, arithmetic and copies ran while one was open for 3% -> 6% of each run, Pallas kernels for 0% -> 0%
where the time goes in v1:
time: 233 us; the launch traced here: 232 us
  Pallas kernels  128 us (55%)
  local copies, waits for them, and re-layouts  50.1 us (22%)
  other arithmetic  19.2 us (8%)
  waiting for transfers between devices  14.6 us (6%)
  matrix products  10.8 us (5%)
  starting transfers between devices  8.11 us (3%)
    pallas_call x3, Pallas kernels, axis_sum(): pl.pallas_call(functools.partial(axis_sum_kernel, axis, gather), out_shap...  53.9 us
    pallas_call x1, Pallas kernels, dp_exchange(): pl.pallas_call(dp_exchange_kernel, out_shape=jax.ShapeDtypeStruct(tiles.s...  35.1 us
    pallas_call x1, Pallas kernels, cache_merged(): pl.pallas_call(cache_kernel, grid_spec=pltpu.PrefetchScalarGridSpec(num_s...  18 us
    pallas_call x1, Pallas kernels, axis_gather(): pl.pallas_call(functools.partial(axis_gather_kernel, axis), out_shape=jax...  15 us
    all_to_all x1, waiting for transfers between devices, shards(): lax.all_to_all(packed(payload, back_index), 'dp', split_axis=0, concat_ax...  14.6 us
    unnamed x44, local copies, waits for them, and re-layouts  13.6 us
    all_to_all x1, starting transfers between devices, shards(): lax.all_to_all(packed(payload, back_index), 'dp', split_axis=0, concat_ax...  8.11 us
    reshape x2, local copies, waits for them, and re-layouts, shards(): cache_values = back[:, :value_width].reshape(local_reqs, tree_slots, GROU...  7.15 us
  transfers between devices with their start and end apart: 1, of which 1 were waited for; matrix products, arithmetic and copies ran while one was open for 6% of the time, Pallas kernels for 0%

profile of v1, /device:TPU:1, one launch (start us, length us, event | category | flops | bytes accessed | tf_op | source)
XLA Modules:
  0.0 231.9 jit_solution(12361519073962545165)
XLA Ops:
  0.7 1.3 multiply_reduce_fusion
  2.7 1.6 fusion.18
  4.5 1.3 reshape.455.x_ref
  5.8 24.3 %shard_map.122 = f32[816,128]{1,0:T(8,128)} custom-call(f32[3264,128]{1,0:T(8,128)} %reshape.455.x_ref), custom_call_target="tpu_custom_call" | custom-call | tf_op jit(solution)/shard_map/pallas_call | solution.py:272
  42.0 15.0 %shard_map.123 = bf16[3072,128]{1,0:T(8,128)(2,1)} custom-call(bf16[768,128]{1,0:T(8,128)(2,1)} %reshape.457.x_ref), custom_call_target="tpu_custom_call" | custom-call | tf_op jit(solution)/shard_map/pallas_call | solution.py:376
  57.0 2.0 reshape.458
  60.2 1.2 gather_fusion
  62.8 35.1 %shard_map.124 = bf16[16,256,128]{2,1,0:T(8,128)(2,1)} custom-call(bf16[16,256,128]{2,1,0:T(8,128)(2,1)} %bitcast_select_fusion.2.x_ref), custom_call_target="tpu_custom_call" | custom-call | tf_op jit(solution)/shard_map/pallas_call | solution.py:322
  97.9 1.9 copy.186
  103.0 1.3 reshape.460.q_ref
  104.3 18.0 %shard_map.125 = (f32[8,2,256]{2,1,0:T(2,128)}, f32[8,2,256]{2,1,0:T(2,128)}, f32[8,256,128]{2,1,0:T(8,128)}) custom-call(s32[8]{0:T(128)} %dynamic_slice.28.lens_ref, s32[1]{0:T(128)} %bitcast.start_ref, bf16[8,256,128]{2,1,0:T(8,128)(2,1)} %reshape.460.q_ref, bf16[8,2048,128]{2,1,0:T(8,128)(2,1)} %k_ref.1, bf16[8,2048,128]{2,1,0:T(8,128)(2,1)} %v_ref.1), custom_call_target="tpu_custom_call" | custom-call | flops 4294967296 | bytes 9961472 | tf_op jit(solution)/shard_map/pallas_call | solution.py:133
  122.3 1.3 reshape.461.x_ref
  123.6 5.8 %shard_map.126 = f32[32,128]{1,0:T(8,128)} custom-call(f32[32,128]{1,0:T(8,128)} %reshape.461.x_ref), custom_call_target="tpu_custom_call" | custom-call | tf_op jit(solution)/shard_map/pallas_call | solution.py:393
  131.3 1.3 multiply_convert_fusion
  133.5 17.8 %shard_map.127 = bf16[2112,128]{1,0:T(8,128)(2,1)} custom-call(bf16[2112,128]{1,0:T(8,128)(2,1)} %fusion.17.x_ref), custom_call_target="tpu_custom_call" | custom-call | tf_op jit(solution)/shard_map/pallas_call | solution.py:272
  152.9 1.3 gather_fusion.2
  154.2 1.1 bitcast_select_fusion.1
  155.8 2.7 %reduce.11 = bf16[16,34816]{1,0:T(8,128)(2,1)S(1)} reduce(bf16[16,1,34816]{2,0,1:T(8,128)(2,1)} %bitcast_select_fusion.1, bf16[]{:T(256)} %broadcast.559), dimensions={1}, to_apply=%copy.131.reduce_sub_computation | reduce | bytes 2228226 | tf_op jit(solution)/shard_map/jit(_take)/select_n | solution.py:68
  158.6 1.7 reshape.524
  160.2 8.1 %all-to-all-start = ((bf16[16,2,17408]{2,1,0:T(2,128)(2,1)}), bf16[16,2,17408]{2,1,0:T(2,128)(2,1)S(1)}, u32[]{:S(2)}, u32[]{:S(2)}) async-start(bf16[16,2,17408]{2,1,0:T(2,128)(2,1)} %reshape.524), calls=%async_computation | async-start | bytes 2228224 | tf_op jit(solution)/shard_map/all_to_all | solution.py:533
  168.3 1.7 fusion.67
  170.8 1.6 reshape.519
  179.7 1.2 fusion.3
  180.9 1.3 copy-done.1
  183.0 14.6 %all-to-all-done = bf16[16,2,17408]{2,1,0:T(2,128)(2,1)S(1)} async-done(((bf16[16,2,17408]{2,1,0:T(2,128)(2,1)}), bf16[16,2,17408]{2,1,0:T(2,128)(2,1)S(1)}, u32[]{:S(2)}, u32[]{:S(2)}) %all-to-all-start) | async-done | bytes 1114144 | tf_op jit(solution)/shard_map/all_to_all | solution.py:533
  197.6 3.4 %reshape.525 = bf16[16,1,34816]{2,1,0:T(2,128)(2,1)} reshape(bf16[16,2,17408]{2,1,0:T(2,128)(2,1)S(1)} %all-to-all-done) | data formatting | bytes 2228224
  201.0 2.3 copy.185
  204.9 2.9 %reshape.468 = f32[8,64,4,2,64]{4,3,2,1,0:T(2,128)} reshape(f32[8,32768]{1,0:T(8,128)S(1)} %slice.99) | data formatting | bytes 2097152 | tf_op jit(solution)/shard_map/reshape | solution.py:540
  207.8 4.3 %copy.132 = f32[8,64,4,2,64]{1,4,2,3,0:T(8,128)} copy(f32[8,64,4,2,64]{4,3,2,1,0:T(2,128)} %reshape.468) | data formatting | bytes 2097152 | tf_op jit(solution)/shard_map/reshape | solution.py:540
  212.1 2.5 %fusion.2 = bf16[8,64,2,4,64]{1,4,3,2,0:T(8,128)(2,1)S(1)} fusion(f32[8,64,4,2,64]{1,4,2,3,0:T(8,128)} %copy.132, f32[8,2,64,64,4]{3,2,4,1,0:T(8,128)S(1)} %copy-done.2, f32[8,64,2,4]{1,3,2,0:T(4,128)S(1)} %get-tuple-element.22, f32[8,64,2,4]{1,3,2,0:T(4,128)S(1)} %get-tuple-element.23, f32[8,64,2,4]{1,3,2,0:T(4,128)S(1)} %copy-done.8, ...), kind=kOutput, calls=%fused_computation.7 | convolution fusion | flops 36175872 | bytes 2850816 | tf_op jit(solution)/shard_map/rtkgu,rukd->rtkgd/dot_general | solution.py:88
  217.5 11.7 %shard_map.128 = f32[512,128]{1,0:T(8,128)} custom-call(bf16[2048,128]{1,0:T(8,128)(2,1)} %convert_element_type.91.x_ref), custom_call_target="tpu_custom_call" | custom-call | tf_op jit(solution)/shard_map/pallas_call | solution.py:272
  230.2 1.7 select_convert_fusion.1
  (147 shorter events, 37.2 us)
Async XLA Ops:
  0.6 2.1 copy-start
  32.2 1.2 copy-start.12
  32.2 2.5 %copy-start.11 = (s32[128,64]{0,1:T(8,128)S(1)}, s32[128,64]{0,1:T(8,128)}, u32[]{:S(2)}) copy-start(s32[128,64]{0,1:T(8,128)} %param.19) | copy-start | bytes 98308
  34.7 3.3 %copy-start.14 = (s32[128]{0:T(128)S(1)}, s32[128]{0:T(128)}, u32[]{:S(2)}) copy-start(s32[128]{0:T(128)} %param.17) | copy-start | bytes 1540
  59.0 0.9 copy-start.5
  132.7 19.8 %copy-start.10 = (f32[32,128]{1,0:T(8,128)S(1)}, f32[32,128]{1,0:T(8,128)}, u32[]{:S(2)}) copy-start(f32[32,128]{1,0:T(8,128)} %shard_map.126) | copy-start | bytes 49156
  151.4 1.4 slice-start
  158.6 12.2 %copy-start.15 = (s32[8]{0:T(128)S(1)}, s32[8]{0:T(128)}, u32[]{:S(2)}) copy-start(s32[8]{0:T(128)} %param.21) | copy-start | bytes 100
  160.2 12.1 %copy-start.3 = (bf16[512,512]{1,0:T(8,128)(2,1)S(1)}, bf16[512,512]{1,0:T(8,128)(2,1)}, u32[]{:S(2)}) copy-start(bf16[512,512]{1,0:T(8,128)(2,1)} %param.11) | copy-start | bytes 1572868
  160.2 37.4 %all-to-all-start = ((bf16[16,2,17408]{2,1,0:T(2,128)(2,1)}), bf16[16,2,17408]{2,1,0:T(2,128)(2,1)S(1)}, u32[]{:S(2)}, u32[]{:S(2)}) async-start(bf16[16,2,17408]{2,1,0:T(2,128)(2,1)} %reshape.524), calls=%async_computation | async-start | bytes 2228224 | tf_op jit(solution)/shard_map/all_to_all | solution.py:533
  172.3 3.4 %copy-start.6 = (bf16[512,128]{1,0:T(8,128)(2,1)S(1)}, bf16[512,128]{1,0:T(8,128)(2,1)}, u32[]{:S(2)}) copy-start(bf16[512,128]{1,0:T(8,128)(2,1)} %get-tuple-element.31) | copy-start | bytes 393220
  172.3 7.2 %copy-start.16 = (s32[8]{0:T(128)S(1)}, s32[8]{0:T(128)}, u32[]{:S(2)}) copy-start(s32[8]{0:T(128)} %param.20) | copy-start | bytes 100
  173.5 6.2 %copy-start.4 = (bf16[8,64,2,4,64]{4,3,2,1,0:T(4,128)(2,1)S(1)}, bf16[8,64,2,4,64]{4,3,2,1,0:T(4,128)(2,1)}, u32[]{:S(2)}) copy-start(bf16[8,64,2,4,64]{4,3,2,1,0:T(4,128)(2,1)} %reshape.519) | copy-start | bytes 1572868
  180.9 1.3 copy-start.1
  180.9 16.7 %copy-start.7 = (f32[8,64,2,4]{1,3,2,0:T(4,128)}, f32[8,64,2,4]{1,3,2,0:T(4,128)S(1)}, u32[]{:S(2)}) copy-start(f32[8,64,2,4]{1,3,2,0:T(4,128)S(1)} %get-tuple-element.43) | copy-start | bytes 49156
  207.8 4.3 %copy-start.8 = (f32[8,64,2,4]{1,3,2,0:T(4,128)S(1)}, f32[8,64,2,4]{1,3,2,0:T(4,128)}, u32[]{:S(2)}) copy-start(f32[8,64,2,4]{1,3,2,0:T(4,128)} %copy-done.7) | copy-start | bytes 49156
  207.8 4.3 %copy-start.2 = (f32[8,2,64,64,4]{3,2,4,1,0:T(8,128)S(1)}, f32[8,2,64,64,4]{3,2,4,1,0:T(8,128)}, u32[]{:S(2)}) copy-start(f32[8,2,64,64,4]{3,2,4,1,0:T(8,128)} %copy-done.1) | copy-start | bytes 3145732
  207.8 4.3 %copy-start.9 = (bf16[8,64,2,64]{1,0,3,2:T(8,128)(2,1)S(1)}, bf16[8,64,2,64]{1,0,3,2:T(8,128)(2,1)}, u32[]{:S(2)}) copy-start(bf16[8,64,2,64]{1,0,3,2:T(8,128)(2,1)} %reshape.472) | copy-start | bytes 393220
  214.6 1.3 copy-start.13

commit v2 on v1

--- a/solution.py
+++ b/solution.py
@@ -79,18 +79,19 @@
 
 def tree_part(queries, keys_new, values_new, ancestors):
     scores = attn_mult * jnp.einsum(
-        "rtkgd,rukd->rtkgu", queries, keys_new, preferred_element_type=jnp.float32
+        "rtkgd,rukd->rtgku", queries, keys_new, preferred_element_type=jnp.float32
     )
     valid_keys = (ancestors > 0.5)[:, :, None, None, :]
     masked = jnp.where(valid_keys, scores, neg_fill)
     top_score = jnp.max(masked, axis=-1)
     weights = jnp.where(valid_keys, jnp.exp(masked - top_score[..., None]), 0.0)
     summed = jnp.einsum(
-        "rtkgu,rukd->rtkgd",
+        "rtgku,rukd->rtgkd",
         weights.astype(jnp.bfloat16),
         values_new,
         preferred_element_type=jnp.float32,
     )
+    summed = summed.reshape(summed.shape[:3] + (-1,))
     return (top_score, jnp.sum(weights, axis=-1), summed)
 
 
@@ -535,15 +536,11 @@
     )
     back = packed(back, send_pos).astype(jnp.float32)
     log_width = log_flat.shape[1]
-    cache_values = (
-        back[:, :value_width]
-        .reshape(local_reqs, tree_slots, GROUP, head_local, HD)
-        .transpose(0, 1, 3, 2, 4)
-    )
+    cache_values = back[:, :value_width].reshape(local_reqs, tree_slots, GROUP, head_local * HD)
     cache_sum = (
         back[:, value_width : value_width + sum_width]
         .reshape(local_reqs, head_local, tree_slots, GROUP)
-        .transpose(0, 2, 1, 3)
+        .transpose(0, 2, 3, 1)
     )
     logs = value_width + sum_width
     cache_top = (
@@ -553,14 +550,23 @@
             + back[:, logs + 2 * log_width :]
         )
         .reshape(local_reqs, head_local, tree_slots, GROUP)
-        .transpose(0, 2, 1, 3)
-    )
-    tree_stats = tree_part(queries, keys_new, values_new, ancestors)
-    top_all, sum_all, summed_all = combine_stats(
-        (cache_top, cache_sum, cache_values), tree_stats
-    )
-    attention = (summed_all / sum_all[..., None]).astype(jnp.bfloat16)
+        .transpose(0, 2, 3, 1)
+    )
+    tree_top, tree_sum, tree_summed = tree_part(queries, keys_new, values_new, ancestors)
+    top_all = jnp.maximum(cache_top, tree_top)
+    scale_cache = jnp.exp(cache_top - top_all)
+    scale_tree = jnp.exp(tree_top - top_all)
+    sum_all = cache_sum * scale_cache + tree_sum * scale_tree
+    summed_all = cache_values * jnp.repeat(scale_cache, HD, axis=-1) + tree_summed * jnp.repeat(
+        scale_tree, HD, axis=-1
+    )
+    attention = (summed_all / jnp.repeat(sum_all, HD, axis=-1)).astype(jnp.bfloat16)
     attention_rows = attention.reshape(row_count, -1)
+    w_out = (
+        w_out.reshape(head_local, GROUP, HD, -1)
+        .transpose(1, 0, 2, 3)
+        .reshape(head_local * GROUP * HD, -1)
+    )
     rows_mine = row_count // lax.axis_size("tx")
     mixed_sum = axis_sum(
         jnp.dot(attention_rows, w_out, preferred_element_type=jnp.float32),

time: 233 us -> 233 us (level)
    reshape x3 -> x2, local copies, waits for them, and re-layouts: 7.76 us -> 7.15 us  [shards(): back[:, :value_width]]
  transfers between devices with their start and end apart: 1 -> 1, of which waited for: 1 -> 1; matrix products, arithmetic and copies ran while one was open for 6% -> 7% of each run, Pallas kernels for 0% -> 0%
where the time goes in v2:
time: 233 us; the launch traced here: 232 us
  Pallas kernels  128 us (55%)
  local copies, waits for them, and re-layouts  51.9 us (22%)
  other arithmetic  19.2 us (8%)
  waiting for transfers between devices  12.8 us (5%)
  matrix products  10.8 us (5%)
  starting transfers between devices  8.01 us (3%)
    pallas_call x3, Pallas kernels, axis_sum(): pl.pallas_call(functools.partial(axis_sum_kernel, axis, gather), out_shap...  53.9 us
    pallas_call x1, Pallas kernels, dp_exchange(): pl.pallas_call(dp_exchange_kernel, out_shape=jax.ShapeDtypeStruct(tiles.s...  35.1 us
    pallas_call x1, Pallas kernels, cache_merged(): pl.pallas_call(cache_kernel, grid_spec=pltpu.PrefetchScalarGridSpec(num_s...  18 us
    pallas_call x1, Pallas kernels, axis_gather(): pl.pallas_call(functools.partial(axis_gather_kernel, axis), out_shape=jax...  15 us
    unnamed x44, local copies, waits for them, and re-layouts  13.6 us
    all_to_all x1, waiting for transfers between devices, shards(): lax.all_to_all(packed(payload, back_index), 'dp', split_axis=0, concat_ax...  12.8 us
    all_to_all x1, starting transfers between devices, shards(): lax.all_to_all(packed(payload, back_index), 'dp', split_axis=0, concat_ax...  8.01 us
    reshape x2, local copies, waits for them, and re-layouts, shards(): back[:, :value_width]  7.15 us
  transfers between devices with their start and end apart: 1, of which 1 were waited for; matrix products, arithmetic and copies ran while one was open for 7% of the time, Pallas kernels for 0%

profile of v2, /device:TPU:1, one launch (start us, length us, event | category | flops | bytes accessed | tf_op | source)
XLA Modules:
  0.0 231.9 jit_solution(7708227990000373982)
XLA Ops:
  0.7 1.3 multiply_reduce_fusion
  2.7 1.6 fusion.18
  4.5 1.3 reshape.467.x_ref
  5.8 24.3 %shard_map.122 = f32[816,128]{1,0:T(8,128)} custom-call(f32[3264,128]{1,0:T(8,128)} %reshape.467.x_ref), custom_call_target="tpu_custom_call" | custom-call | tf_op jit(solution)/shard_map/pallas_call | solution.py:273
  42.0 15.0 %shard_map.123 = bf16[3072,128]{1,0:T(8,128)(2,1)} custom-call(bf16[768,128]{1,0:T(8,128)(2,1)} %reshape.469.x_ref), custom_call_target="tpu_custom_call" | custom-call | tf_op jit(solution)/shard_map/pallas_call | solution.py:377
  57.0 2.0 reshape.470
  60.2 1.2 gather_fusion
  62.8 35.1 %shard_map.124 = bf16[16,256,128]{2,1,0:T(8,128)(2,1)} custom-call(bf16[16,256,128]{2,1,0:T(8,128)(2,1)} %bitcast_select_fusion.2.x_ref), custom_call_target="tpu_custom_call" | custom-call | tf_op jit(solution)/shard_map/pallas_call | solution.py:323
  97.9 1.9 copy.216
  103.0 1.3 reshape.472.q_ref
  104.3 18.0 %shard_map.125 = (f32[8,2,256]{2,1,0:T(2,128)}, f32[8,2,256]{2,1,0:T(2,128)}, f32[8,256,128]{2,1,0:T(8,128)}) custom-call(s32[8]{0:T(128)} %dynamic_slice.28.lens_ref, s32[1]{0:T(128)} %bitcast.start_ref, bf16[8,256,128]{2,1,0:T(8,128)(2,1)} %reshape.472.q_ref, bf16[8,2048,128]{2,1,0:T(8,128)(2,1)} %k_ref.1, bf16[8,2048,128]{2,1,0:T(8,128)(2,1)} %v_ref.1), custom_call_target="tpu_custom_call" | custom-call | flops 4294967296 | bytes 9961472 | tf_op jit(solution)/shard_map/pallas_call | solution.py:134
  122.3 1.3 reshape.473.x_ref
  123.6 5.8 %shard_map.126 = f32[32,128]{1,0:T(8,128)} custom-call(f32[32,128]{1,0:T(8,128)} %reshape.473.x_ref), custom_call_target="tpu_custom_call" | custom-call | tf_op jit(solution)/shard_map/pallas_call | solution.py:394
  131.3 1.3 multiply_convert_fusion
  133.5 17.8 %shard_map.127 = bf16[2112,128]{1,0:T(8,128)(2,1)} custom-call(bf16[2112,128]{1,0:T(8,128)(2,1)} %fusion.17.x_ref), custom_call_target="tpu_custom_call" | custom-call | tf_op jit(solution)/shard_map/pallas_call | solution.py:273
  152.9 1.3 gather_fusion.2
  155.8 2.7 %reduce.11 = bf16[16,34816]{1,0:T(8,128)(2,1)S(1)} reduce(bf16[16,1,34816]{2,0,1:T(8,128)(2,1)} %bitcast_select_fusion.1, bf16[]{:T(256)} %broadcast.556), dimensions={1}, to_apply=%copy.160.reduce_sub_computation | reduce | bytes 2228226 | tf_op jit(solution)/shard_map/jit(_take)/select_n | solution.py:68
  158.6 1.7 reshape.537
  160.2 8.0 %all-to-all-start = ((bf16[16,2,17408]{2,1,0:T(2,128)(2,1)}), bf16[16,2,17408]{2,1,0:T(2,128)(2,1)S(1)}, u32[]{:S(2)}, u32[]{:S(2)}) async-start(bf16[16,2,17408]{2,1,0:T(2,128)(2,1)} %reshape.537), calls=%async_computation | async-start | bytes 2228224 | tf_op jit(solution)/shard_map/all_to_all | solution.py:534
  168.2 1.7 fusion.67
  170.7 1.6 reshape.532
  176.7 1.9 copy.174
  181.5 1.2 fusion.3
  182.7 1.3 copy-done.1
  184.7 12.8 %all-to-all-done = bf16[16,2,17408]{2,1,0:T(2,128)(2,1)S(1)} async-done(((bf16[16,2,17408]{2,1,0:T(2,128)(2,1)}), bf16[16,2,17408]{2,1,0:T(2,128)(2,1)S(1)}, u32[]{:S(2)}, u32[]{:S(2)}) %all-to-all-start) | async-done | bytes 1114144 | tf_op jit(solution)/shard_map/all_to_all | solution.py:534
  197.5 3.4 %reshape.538 = bf16[16,1,34816]{2,1,0:T(2,128)(2,1)} reshape(bf16[16,2,17408]{2,1,0:T(2,128)(2,1)S(1)} %all-to-all-done) | data formatting | bytes 2228224
  200.9 2.3 copy.215
  204.8 2.9 %reshape.480 = f32[8,64,4,2,64]{4,3,2,1,0:T(2,128)} reshape(f32[8,32768]{1,0:T(8,128)S(1)} %slice.99) | data formatting | bytes 2097152 | tf_op jit(solution)/shard_map/reshape | solution.py:539
  207.7 4.3 %copy.167 = f32[8,64,4,2,64]{1,4,2,3,0:T(8,128)} copy(f32[8,64,4,2,64]{4,3,2,1,0:T(2,128)} %reshape.480) | data formatting | bytes 2097152 | tf_op jit(solution)/shard_map/reshape | solution.py:539
  212.0 2.5 %fusion.2 = bf16[8,64,4,2,64]{1,4,2,3,0:T(8,128)(2,1)S(1)} fusion(f32[8,64,4,2,64]{1,4,2,3,0:T(8,128)} %copy.167, f32[8,2,64,64,4]{3,2,4,1,0:T(8,128)S(1)} %copy-done.2, f32[8,64,4,2]{1,2,3,0:T(4,128)S(1)} %get-tuple-element.24, f32[8,64,4,2]{1,2,3,0:T(4,128)S(1)} %get-tuple-element.25, f32[8,64,4,2]{1,2,3,0:T(4,128)S(1)} %copy-done.9, ...), kind=kOutput, calls=%fused_computation.7 | convolution fusion | flops 36175872 | bytes 2850816 | tf_op jit(solution)/shard_map/rtgku,rukd->rtgkd/dot_general | solution.py:88
  217.4 11.8 %shard_map.128 = f32[512,128]{1,0:T(8,128)} custom-call(bf16[2048,128]{1,0:T(8,128)(2,1)} %convert_element_type.96.x_ref), custom_call_target="tpu_custom_call" | custom-call | tf_op jit(solution)/shard_map/pallas_call | solution.py:273
  230.2 1.7 select_convert_fusion.1
  (148 shorter events, 38.4 us)
Async XLA Ops:
  0.6 2.1 copy-start
  32.2 1.2 copy-start.13
  32.2 2.5 %copy-start.12 = (s32[128,64]{0,1:T(8,128)S(1)}, s32[128,64]{0,1:T(8,128)}, u32[]{:S(2)}) copy-start(s32[128,64]{0,1:T(8,128)} %param.19) | copy-start | bytes 98308
  34.7 3.3 %copy-start.14 = (s32[128]{0:T(128)S(1)}, s32[128]{0:T(128)}, u32[]{:S(2)}) copy-start(s32[128]{0:T(128)} %param.17) | copy-start | bytes 1540
  59.0 0.9 copy-start.5
  132.7 19.8 %copy-start.11 = (f32[32,128]{1,0:T(8,128)S(1)}, f32[32,128]{1,0:T(8,128)}, u32[]{:S(2)}) copy-start(f32[32,128]{1,0:T(8,128)} %shard_map.126) | copy-start | bytes 49156
  151.4 1.4 slice-start
  158.6 12.1 %copy-start.15 = (s32[8]{0:T(128)S(1)}, s32[8]{0:T(128)}, u32[]{:S(2)}) copy-start(s32[8]{0:T(128)} %param.21) | copy-start | bytes 100
  160.2 12.0 %copy-start.3 = (bf16[512,512]{1,0:T(8,128)(2,1)S(1)}, bf16[512,512]{1,0:T(8,128)(2,1)}, u32[]{:S(2)}) copy-start(bf16[512,512]{1,0:T(8,128)(2,1)} %param.11) | copy-start | bytes 1572868
  160.2 37.3 %all-to-all-start = ((bf16[16,2,17408]{2,1,0:T(2,128)(2,1)}), bf16[16,2,17408]{2,1,0:T(2,128)(2,1)S(1)}, u32[]{:S(2)}, u32[]{:S(2)}) async-start(bf16[16,2,17408]{2,1,0:T(2,128)(2,1)} %reshape.537), calls=%async_computation | async-start | bytes 2228224 | tf_op jit(solution)/shard_map/all_to_all | solution.py:534
  172.2 3.4 %copy-start.7 = (bf16[512,128]{1,0:T(8,128)(2,1)S(1)}, bf16[512,128]{1,0:T(8,128)(2,1)}, u32[]{:S(2)}) copy-start(bf16[512,128]{1,0:T(8,128)(2,1)} %get-tuple-element.33) | copy-start | bytes 393220
  172.3 9.1 %copy-start.16 = (s32[8]{0:T(128)S(1)}, s32[8]{0:T(128)}, u32[]{:S(2)}) copy-start(s32[8]{0:T(128)} %param.20) | copy-start | bytes 100
  173.4 8.1 %copy-start.4 = (bf16[8,64,2,4,64]{4,3,2,1,0:T(4,128)(2,1)S(1)}, bf16[8,64,2,4,64]{4,3,2,1,0:T(4,128)(2,1)}, u32[]{:S(2)}) copy-start(bf16[8,64,2,4,64]{4,3,2,1,0:T(4,128)(2,1)} %reshape.532) | copy-start | bytes 1572868
  182.7 1.3 copy-start.1
  182.7 14.8 %copy-start.8 = (f32[8,64,4,2]{1,2,3,0:T(4,128)}, f32[8,64,4,2]{1,2,3,0:T(4,128)S(1)}, u32[]{:S(2)}) copy-start(f32[8,64,4,2]{1,2,3,0:T(4,128)S(1)} %get-tuple-element.45) | copy-start | bytes 49156
  207.7 4.3 %copy-start.9 = (f32[8,64,4,2]{1,2,3,0:T(4,128)S(1)}, f32[8,64,4,2]{1,2,3,0:T(4,128)}, u32[]{:S(2)}) copy-start(f32[8,64,4,2]{1,2,3,0:T(4,128)} %copy-done.8) | copy-start | bytes 49156
  207.7 4.3 %copy-start.2 = (f32[8,2,64,64,4]{3,2,4,1,0:T(8,128)S(1)}, f32[8,2,64,64,4]{3,2,4,1,0:T(8,128)}, u32[]{:S(2)}) copy-start(f32[8,2,64,64,4]{3,2,4,1,0:T(8,128)} %copy-done.1) | copy-start | bytes 3145732
  207.7 4.3 %copy-start.10 = (bf16[8,64,2,64]{1,0,3,2:T(8,128)(2,1)S(1)}, bf16[8,64,2,64]{1,0,3,2:T(8,128)(2,1)}, u32[]{:S(2)}) copy-start(bf16[8,64,2,64]{1,0,3,2:T(8,128)(2,1)} %reshape.484) | copy-start | bytes 393220
  214.5 1.3 copy-start.6

commit v3 on v1

--- a/solution.py
+++ b/solution.py
@@ -65,7 +65,10 @@
 
 
 def packed(values, index):
-    return jnp.take(values, index, axis=0, mode="fill", fill_value=0)
+    chooser = (index[:, None] == jnp.arange(values.shape[0], dtype=index.dtype)[None, :]).astype(
+        values.dtype
+    )
+    return jnp.dot(chooser, values, preferred_element_type=jnp.float32).astype(values.dtype)
 
 
 def routing(home_slot, group_count, local_reqs):
@@ -530,9 +533,10 @@
         ],
         axis=1,
     )
+    outgoing = packed(payload, back_index)
     back = lax.all_to_all(
-        packed(payload, back_index), "dp", split_axis=0, concat_axis=0, tiled=True
-    )
+        outgoing.reshape(outgoing.shape[0], -1, 128), "dp", split_axis=0, concat_axis=0, tiled=True
+    ).reshape(outgoing.shape)
     back = packed(back, send_pos).astype(jnp.float32)
     log_width = log_flat.shape[1]
     cache_values = (

time: 233 us -> 224 us (0.961)
  local copies, waits for them, and re-layouts: 50.1 us -> 37.8 us
  other arithmetic: 19.2 us -> 13.4 us
  waiting for transfers between devices: 14.6 us -> 20 us
  matrix products: 10.8 us -> 14.7 us
    unnamed x44 -> x35, local copies, waits for them, and re-layouts: 13.6 us -> 3.37 us
    gather x5 -> x0, local copies, waits for them, and re-layouts: 5.43 us -> none  [packed(): return jnp.take(values, index, axis=0, mode='fill', fill_value=0)]
    all_to_all x1, waiting for transfers between devices: 14.6 us -> 20 us  [shards(): lax.all_to_all(outgoing.reshape(outgoing.shape[0], -1, 128), 'dp', split_...]
    select_n x7 -> x2, other arithmetic: 5.04 us -> 0.01 us  [the longest x1 0.01 us: shards(): jnp.where(jnp.any(back_hit, axis=1), jnp.sum(jnp.where(back_hit, local_id...]
    dot_general x0 -> x4, matrix products: none -> 4.48 us  [packed(): jnp.dot(chooser, values, preferred_element_type=jnp.float32)]
  transfers between devices with their start and end apart: 1 -> 1, of which waited for: 1 -> 1; matrix products, arithmetic and copies ran while one was open for 6% -> 4% of each run, Pallas kernels for 0% -> 0%
where the time goes in v3:
time: 224 us; the launch traced here: 223 us
  Pallas kernels  128 us (57%)
  local copies, waits for them, and re-layouts  37.8 us (17%)
  waiting for transfers between devices  20 us (9%)
  matrix products  14.7 us (7%)
  other arithmetic  13.4 us (6%)
  starting transfers between devices  8.13 us (4%)
    pallas_call x3, Pallas kernels, axis_sum(): pl.pallas_call(functools.partial(axis_sum_kernel, axis, gather), out_shap...  53.8 us
    pallas_call x1, Pallas kernels, dp_exchange(): pl.pallas_call(dp_exchange_kernel, out_shape=jax.ShapeDtypeStruct(tiles.s...  35.1 us
    all_to_all x1, waiting for transfers between devices, shards(): lax.all_to_all(outgoing.reshape(outgoing.shape[0], -1, 128), 'dp', split_...  20 us
    pallas_call x1, Pallas kernels, cache_merged(): pl.pallas_call(cache_kernel, grid_spec=pltpu.PrefetchScalarGridSpec(num_s...  18 us
    pallas_call x1, Pallas kernels, axis_gather(): pl.pallas_call(functools.partial(axis_gather_kernel, axis), out_shape=jax...  15 us
    reshape x2, local copies, waits for them, and re-layouts, shards(): cache_values = back[:, :value_width].reshape(local_reqs, tree_slots, GROU...  8.24 us
    all_to_all x1, starting transfers between devices, shards(): lax.all_to_all(outgoing.reshape(outgoing.shape[0], -1, 128), 'dp', split_...  8.13 us
    pallas_call x1, Pallas kernels, ty_max(): pl.pallas_call(ty_max_kernel, out_shape=jax.ShapeDtypeStruct(flat.shape,...  5.78 us
  transfers between devices with their start and end apart: 1, of which 1 were waited for; matrix products, arithmetic and copies ran while one was open for 4% of the time, Pallas kernels for 0%

profile of v3, /device:TPU:1, one launch (start us, length us, event | category | flops | bytes accessed | tf_op | source)
XLA Modules:
  0.0 223.0 jit_solution(1558348201914751083)
XLA Ops:
  0.7 1.3 multiply_reduce_fusion
  2.7 1.6 fusion.24
  4.5 1.3 reshape.307.x_ref
  5.8 24.3 %shard_map.122 = f32[816,128]{1,0:T(8,128)} custom-call(f32[3264,128]{1,0:T(8,128)} %reshape.307.x_ref), custom_call_target="tpu_custom_call" | custom-call | tf_op jit(solution)/shard_map/pallas_call | solution.py:275
  31.1 1.1 reshape.308
  36.3 1.1 fusion.37
  41.4 15.0 %shard_map.123 = bf16[3072,128]{1,0:T(8,128)(2,1)} custom-call(bf16[768,128]{1,0:T(8,128)(2,1)} %reshape.309.x_ref), custom_call_target="tpu_custom_call" | custom-call | tf_op jit(solution)/shard_map/pallas_call | solution.py:379
  56.5 2.0 reshape.310
  59.2 1.2 copy.165
  60.4 35.1 %shard_map.124 = bf16[16,256,128]{2,1,0:T(8,128)(2,1)} custom-call(bf16[16,256,128]{2,1,0:T(8,128)(2,1)} %bitcast.98), custom_call_target="tpu_custom_call" | custom-call | tf_op jit(solution)/shard_map/pallas_call | solution.py:325
  95.8 1.9 convolution_convert_fusion.3
  97.7 1.1 reshape.313
  100.0 1.3 reshape.314.q_ref
  101.3 18.0 %shard_map.125 = (f32[8,2,256]{2,1,0:T(2,128)}, f32[8,2,256]{2,1,0:T(2,128)}, f32[8,256,128]{2,1,0:T(8,128)}) custom-call(s32[8]{0:T(128)} %dynamic_slice.28.lens_ref, s32[1]{0:T(128)} %bitcast.start_ref, bf16[8,256,128]{2,1,0:T(8,128)(2,1)} %reshape.314.q_ref, bf16[8,2048,128]{2,1,0:T(8,128)(2,1)} %k_ref.1, bf16[8,2048,128]{2,1,0:T(8,128)(2,1)} %v_ref.1), custom_call_target="tpu_custom_call" | custom-call | flops 4294967296 | bytes 9961472 | tf_op jit(solution)/shard_map/pallas_call | solution.py:136
  119.3 1.3 reshape.315.x_ref
  120.6 5.8 %shard_map.126 = f32[32,128]{1,0:T(8,128)} custom-call(f32[32,128]{1,0:T(8,128)} %reshape.315.x_ref), custom_call_target="tpu_custom_call" | custom-call | tf_op jit(solution)/shard_map/pallas_call | solution.py:396
  128.3 1.3 multiply_convert_fusion
  130.5 17.8 %shard_map.127 = bf16[2112,128]{1,0:T(8,128)(2,1)} custom-call(bf16[2112,128]{1,0:T(8,128)(2,1)} %fusion.23.x_ref), custom_call_target="tpu_custom_call" | custom-call | tf_op jit(solution)/shard_map/pallas_call | solution.py:275
  148.4 1.1 slice.74
  150.5 1.2 copy.167
  151.7 8.1 %all-to-all-start = ((bf16[16,272,128]{2,1,0:T(8,128)(2,1)}), bf16[16,272,128]{2,1,0:T(8,128)(2,1)}, u32[]{:S(2)}, u32[]{:S(2)}) async-start(bf16[16,272,128]{2,1,0:T(8,128)(2,1)} %bitcast.30), calls=%async_computation | async-start | bytes 2228224 | tf_op jit(solution)/shard_map/all_to_all | solution.py:537
  159.9 1.5 reshape.342
  161.4 1.1 convert_element_type.91
  166.1 2.4 %fusion.4 = (f32[8,64,2,4]{1,3,2,0:T(4,128)S(1)}, f32[8,2,64,64,4]{3,2,4,1,0:T(8,128)S(1)}) fusion(pred[8,64,64]{1,2,0:T(8,128)(4,1)S(1)} %copy.135, bf16[8,64,2,4,64]{4,3,2,1,0:T(4,128)(2,1)} %reshape.342, bf16[8,64,2,64,1]{1,0,3,2,4:T(8,128)(2,1)S(1)} %bitcast.105), kind=kOutput, calls=%fused_computation.12 | convolution fusion | flops 34336768 | bytes 1753088 | tf_op jit(solution)/shard_map/rtkgd,rukd->rtkgu/dot_general | solution.py:84
  169.2 20.0 %all-to-all-done = bf16[16,272,128]{2,1,0:T(8,128)(2,1)} async-done(((bf16[16,272,128]{2,1,0:T(8,128)(2,1)}), bf16[16,272,128]{2,1,0:T(8,128)(2,1)}, u32[]{:S(2)}, u32[]{:S(2)}) %all-to-all-start) | async-done | bytes 1114144 | tf_op jit(solution)/shard_map/all_to_all | solution.py:537
  189.2 1.6 fusion
  194.9 4.1 %reshape.324 = f32[8,64,4,2,64]{4,3,2,1,0:T(2,128)} reshape(f32[8,32768]{1,0:T(8,128)} %slice.91) | data formatting | bytes 2097152 | tf_op jit(solution)/shard_map/reshape | solution.py:544
  199.0 4.1 %copy.132 = f32[8,64,4,2,64]{1,4,2,3,0:T(8,128)} copy(f32[8,64,4,2,64]{4,3,2,1,0:T(2,128)} %reshape.324) | data formatting | bytes 2097152 | tf_op jit(solution)/shard_map/reshape | solution.py:544
  203.2 2.5 %fusion.3 = bf16[8,64,2,4,64]{1,4,3,2,0:T(8,128)(2,1)S(1)} fusion(f32[8,64,4,2,64]{1,4,2,3,0:T(8,128)} %copy.132, f32[8,2,64,64,4]{3,2,4,1,0:T(8,128)S(1)} %get-tuple-element.42, f32[8,64,2,4]{1,3,2,0:T(4,128)S(1)} %get-tuple-element.22, f32[8,64,2,4]{1,3,2,0:T(4,128)S(1)} %get-tuple-element.23, f32[8,64,2,4]{1,3,2,0:T(4,128)S(1)} %get-tuple-element.41, ...), kind=kOutput, calls=%fused_computation.8 | convolution fusion | flops 36175872 | bytes 2850816 | tf_op jit(solution)/shard_map/rtkgu,rukd->rtkgd/dot_general | solution.py:91
  207.5 1.1 convert_element_type.111.x_ref
  208.6 11.7 %shard_map.128 = f32[512,128]{1,0:T(8,128)} custom-call(bf16[2048,128]{1,0:T(8,128)(2,1)} %convert_element_type.111.x_ref), custom_call_target="tpu_custom_call" | custom-call | tf_op jit(solution)/shard_map/pallas_call | solution.py:275
  221.3 1.7 select_convert_fusion
  (125 shorter events, 26.9 us)
Async XLA Ops:
  0.6 2.1 copy-start
  32.2 1.2 copy-start.8
  32.2 2.0 copy-start.7
  34.2 3.4 %copy-start.11 = (s32[128]{0:T(128)S(1)}, s32[128]{0:T(128)}, u32[]{:S(2)}) copy-start(s32[128]{0:T(128)} %param.17) | copy-start | bytes 1540
  58.4 2.0 copy-start.2
  129.7 19.8 %copy-start.3 = (f32[32,128]{1,0:T(8,128)S(1)}, f32[32,128]{1,0:T(8,128)}, u32[]{:S(2)}) copy-start(f32[32,128]{1,0:T(8,128)} %shard_map.126) | copy-start | bytes 49156
  148.4 1.6 slice-start
  151.7 9.7 %copy-start.1 = (bf16[512,512]{1,0:T(8,128)(2,1)S(1)}, bf16[512,512]{1,0:T(8,128)(2,1)}, u32[]{:S(2)}) copy-start(bf16[512,512]{1,0:T(8,128)(2,1)} %param.11) | copy-start | bytes 1572868
  151.7 37.5 %all-to-all-start = ((bf16[16,272,128]{2,1,0:T(8,128)(2,1)}), bf16[16,272,128]{2,1,0:T(8,128)(2,1)}, u32[]{:S(2)}, u32[]{:S(2)}) async-start(bf16[16,272,128]{2,1,0:T(8,128)(2,1)} %bitcast.30), calls=%async_computation | async-start | bytes 2228224 | tf_op jit(solution)/shard_map/all_to_all | solution.py:537
  161.4 3.0 %copy-start.12 = (s32[8]{0:T(128)S(1)}, s32[8]{0:T(128)}, u32[]{:S(2)}) copy-start(s32[8]{0:T(128)} %param.21) | copy-start | bytes 100
  161.4 3.1 %copy-start.6 = (bf16[8,64,64]{2,1,0:T(8,128)(2,1)S(1)}, bf16[8,64,64]{2,1,0:T(8,128)(2,1)}, u32[]{:S(2)}) copy-start(bf16[8,64,64]{2,1,0:T(8,128)(2,1)} %get-tuple-element.40) | copy-start | bytes 196612
  161.4 4.0 %copy-start.13 = (s32[8]{0:T(128)S(1)}, s32[8]{0:T(128)}, u32[]{:S(2)}) copy-start(s32[8]{0:T(128)} %param.20) | copy-start | bytes 100
  199.0 4.2 %copy-start.4 = (f32[8,2,64,4]{2,3,1,0:T(4,128)S(1)}, f32[8,2,64,4]{2,3,1,0:T(4,128)}, u32[]{:S(2)}) copy-start(f32[8,2,64,4]{2,3,1,0:T(4,128)} %copy.134) | copy-start | bytes 49156
  199.0 4.2 %copy-start.5 = (f32[8,2,64,4]{2,3,1,0:T(4,128)S(1)}, f32[8,2,64,4]{2,3,1,0:T(4,128)}, u32[]{:S(2)}) copy-start(f32[8,2,64,4]{2,3,1,0:T(4,128)} %copy.143) | copy-start | bytes 49156
  205.7 1.3 copy-start.10
  207.0 14.3 %copy-start.9 = (pred[128]{0:T(512)(128)(4,1)S(1)}, pred[128]{0:T(512)(128)(4,1)}, u32[]{:S(2)}) copy-start(pred[128]{0:T(512)(128)(4,1)} %fusion.59) | copy-start | bytes 388

commit v4 on v3

--- a/solution.py
+++ b/solution.py
@@ -525,7 +525,9 @@
     log_low = log_rest - log_mid
     payload = jnp.concatenate(
         [
-            summed,
+            summed.reshape(local_reqs, tree_slots, GROUP, head_local, HD)
+            .transpose(0, 1, 3, 2, 4)
+            .reshape(local_reqs, -1),
             weight_sum,
             log_high.astype(jnp.bfloat16),
             log_mid.astype(jnp.bfloat16),
@@ -539,11 +541,7 @@
     ).reshape(outgoing.shape)
     back = packed(back, send_pos).astype(jnp.float32)
     log_width = log_flat.shape[1]
-    cache_values = (
-        back[:, :value_width]
-        .reshape(local_reqs, tree_slots, GROUP, head_local, HD)
-        .transpose(0, 1, 3, 2, 4)
-    )
+    cache_values = back[:, :value_width].reshape(local_reqs, tree_slots, head_local, GROUP, HD)
     cache_sum = (
         back[:, value_width : value_width + sum_width]
         .reshape(local_reqs, head_local, tree_slots, GROUP)

time: 224 us -> 224 us (level)
  no operation moved by 1% of the time
where the time goes in v4:
time: 224 us; the launch traced here: 223 us
  Pallas kernels  128 us (57%)
  local copies, waits for them, and re-layouts  37.9 us (17%)
  waiting for transfers between devices  20 us (9%)
  matrix products  14.7 us (7%)
  other arithmetic  13.4 us (6%)
  starting transfers between devices  8.13 us (4%)
    pallas_call x3, Pallas kernels, axis_sum(): pl.pallas_call(functools.partial(axis_sum_kernel, axis, gather), out_shap...  53.8 us
    pallas_call x1, Pallas kernels, dp_exchange(): pl.pallas_call(dp_exchange_kernel, out_shape=jax.ShapeDtypeStruct(tiles.s...  35.1 us
    all_to_all x1, waiting for transfers between devices, shards(): lax.all_to_all(outgoing.reshape(outgoing.shape[0], -1, 128), 'dp', split_...  20 us
    pallas_call x1, Pallas kernels, cache_merged(): pl.pallas_call(cache_kernel, grid_spec=pltpu.PrefetchScalarGridSpec(num_s...  18 us
    pallas_call x1, Pallas kernels, axis_gather(): pl.pallas_call(functools.partial(axis_gather_kernel, axis), out_shape=jax...  15 us
    all_to_all x1, starting transfers between devices, shards(): lax.all_to_all(outgoing.reshape(outgoing.shape[0], -1, 128), 'dp', split_...  8.13 us
    reshape x2, local copies, waits for them, and re-layouts, shards(): back[:, :value_width].reshape(local_reqs, tree_slots, head_local, GROUP, HD)  6.9 us
    pallas_call x1, Pallas kernels, ty_max(): pl.pallas_call(ty_max_kernel, out_shape=jax.ShapeDtypeStruct(flat.shape,...  5.78 us
  transfers between devices with their start and end apart: 1, of which 1 were waited for; matrix products, arithmetic and copies ran while one was open for 4% of the time, Pallas kernels for 0%

profile of v4, /device:TPU:1, one launch (start us, length us, event | category | flops | bytes accessed | tf_op | source)
XLA Modules:
  0.0 223.0 jit_solution(15712375361537143612)
XLA Ops:
  0.7 1.3 multiply_reduce_fusion
  2.7 1.6 fusion.24
  4.5 1.3 reshape.307.x_ref
  5.8 24.3 %shard_map.122 = f32[816,128]{1,0:T(8,128)} custom-call(f32[3264,128]{1,0:T(8,128)} %reshape.307.x_ref), custom_call_target="tpu_custom_call" | custom-call | tf_op jit(solution)/shard_map/pallas_call | solution.py:275
  31.1 1.1 reshape.308
  36.3 1.1 fusion.37
  41.4 15.0 %shard_map.123 = bf16[3072,128]{1,0:T(8,128)(2,1)} custom-call(bf16[768,128]{1,0:T(8,128)(2,1)} %reshape.309.x_ref), custom_call_target="tpu_custom_call" | custom-call | tf_op jit(solution)/shard_map/pallas_call | solution.py:379
  56.5 2.0 reshape.310
  59.2 1.2 copy.170
  60.4 35.1 %shard_map.124 = bf16[16,256,128]{2,1,0:T(8,128)(2,1)} custom-call(bf16[16,256,128]{2,1,0:T(8,128)(2,1)} %bitcast.97), custom_call_target="tpu_custom_call" | custom-call | tf_op jit(solution)/shard_map/pallas_call | solution.py:325
  95.8 1.9 convolution_convert_fusion.3
  97.7 1.1 reshape.313
  98.9 1.1 copy.197
  100.0 1.3 reshape.314.q_ref
  101.3 18.0 %shard_map.125 = (f32[8,2,256]{2,1,0:T(2,128)}, f32[8,2,256]{2,1,0:T(2,128)}, f32[8,256,128]{2,1,0:T(8,128)}) custom-call(s32[8]{0:T(128)} %dynamic_slice.28.lens_ref, s32[1]{0:T(128)} %bitcast.start_ref, bf16[8,256,128]{2,1,0:T(8,128)(2,1)} %reshape.314.q_ref, bf16[8,2048,128]{2,1,0:T(8,128)(2,1)} %k_ref.1, bf16[8,2048,128]{2,1,0:T(8,128)(2,1)} %v_ref.1), custom_call_target="tpu_custom_call" | custom-call | flops 4294967296 | bytes 9961472 | tf_op jit(solution)/shard_map/pallas_call | solution.py:136
  119.3 1.3 reshape.315.x_ref
  120.6 5.8 %shard_map.126 = f32[32,128]{1,0:T(8,128)} custom-call(f32[32,128]{1,0:T(8,128)} %reshape.315.x_ref), custom_call_target="tpu_custom_call" | custom-call | tf_op jit(solution)/shard_map/pallas_call | solution.py:396
  128.3 1.3 multiply_convert_fusion
  130.5 17.8 %shard_map.127 = bf16[2112,128]{1,0:T(8,128)(2,1)} custom-call(bf16[2112,128]{1,0:T(8,128)(2,1)} %fusion.23.x_ref), custom_call_target="tpu_custom_call" | custom-call | tf_op jit(solution)/shard_map/pallas_call | solution.py:275
  151.9 1.2 copy.172
  153.1 8.1 %all-to-all-start = ((bf16[16,272,128]{2,1,0:T(8,128)(2,1)}), bf16[16,272,128]{2,1,0:T(8,128)(2,1)}, u32[]{:S(2)}, u32[]{:S(2)}) async-start(bf16[16,272,128]{2,1,0:T(8,128)(2,1)} %bitcast.30), calls=%async_computation | async-start | bytes 2228224 | tf_op jit(solution)/shard_map/all_to_all | solution.py:539
  161.2 1.5 reshape.342
  162.8 1.1 convert_element_type.91
  167.5 2.4 %fusion.4 = (f32[8,64,2,4]{1,3,2,0:T(4,128)S(1)}, f32[8,2,64,64,4]{3,2,4,1,0:T(8,128)S(1)}) fusion(pred[8,64,64]{1,2,0:T(8,128)(4,1)S(1)} %copy.139, bf16[8,64,2,4,64]{4,3,2,1,0:T(4,128)(2,1)} %reshape.342, bf16[8,64,2,64,1]{1,0,3,2,4:T(8,128)(2,1)S(1)} %bitcast.105), kind=kOutput, calls=%fused_computation.11 | convolution fusion | flops 34336768 | bytes 1753088 | tf_op jit(solution)/shard_map/rtkgd,rukd->rtkgu/dot_general | solution.py:84
  170.6 20.0 %all-to-all-done = bf16[16,272,128]{2,1,0:T(8,128)(2,1)} async-done(((bf16[16,272,128]{2,1,0:T(8,128)(2,1)}), bf16[16,272,128]{2,1,0:T(8,128)(2,1)}, u32[]{:S(2)}, u32[]{:S(2)}) %all-to-all-start) | async-done | bytes 1114144 | tf_op jit(solution)/shard_map/all_to_all | solution.py:539
  190.6 1.6 fusion
  196.3 4.0 %reshape.324 = f32[8,64,2,4,64]{4,3,2,1,0:T(4,128)} reshape(f32[8,32768]{1,0:T(8,128)} %slice.91) | data formatting | bytes 2097152 | tf_op jit(solution)/shard_map/reshape | solution.py:544
  200.3 2.9 %copy.143 = f32[8,64,2,4,64]{1,4,3,2,0:T(8,128)} copy(f32[8,64,2,4,64]{4,3,2,1,0:T(4,128)} %reshape.324) | data formatting | bytes 2097152 | tf_op jit(solution)/shard_map/reshape | solution.py:544
  203.3 2.5 %fusion.3 = bf16[8,64,2,4,64]{1,4,3,2,0:T(8,128)(2,1)S(1)} fusion(f32[8,64,2,4,64]{1,4,3,2,0:T(8,128)} %copy.143, f32[8,2,64,64,4]{3,2,4,1,0:T(8,128)S(1)} %get-tuple-element.42, f32[8,64,2,4]{1,3,2,0:T(4,128)S(1)} %get-tuple-element.22, f32[8,64,2,4]{1,3,2,0:T(4,128)S(1)} %get-tuple-element.23, f32[8,64,2,4]{1,3,2,0:T(4,128)S(1)} %get-tuple-element.41, ...), kind=kOutput, calls=%fused_computation.8 | convolution fusion | flops 36175872 | bytes 2850816 | tf_op jit(solution)/shard_map/rtkgu,rukd->rtkgd/dot_general | solution.py:91
  207.5 1.1 convert_element_type.111.x_ref
  208.6 11.7 %shard_map.128 = f32[512,128]{1,0:T(8,128)} custom-call(bf16[2048,128]{1,0:T(8,128)(2,1)} %convert_element_type.111.x_ref), custom_call_target="tpu_custom_call" | custom-call | tf_op jit(solution)/shard_map/pallas_call | solution.py:275
  221.3 1.7 select_convert_fusion
  (127 shorter events, 28.3 us)
Async XLA Ops:
  0.6 2.1 copy-start
  32.2 1.2 copy-start.8
  32.2 2.0 copy-start.7
  34.2 3.4 %copy-start.11 = (s32[128]{0:T(128)S(1)}, s32[128]{0:T(128)}, u32[]{:S(2)}) copy-start(s32[128]{0:T(128)} %param.17) | copy-start | bytes 1540
  58.4 2.0 copy-start.2
  129.7 19.8 %copy-start.3 = (f32[32,128]{1,0:T(8,128)S(1)}, f32[32,128]{1,0:T(8,128)}, u32[]{:S(2)}) copy-start(f32[32,128]{1,0:T(8,128)} %shard_map.126) | copy-start | bytes 49156
  150.0 1.3 slice-start
  153.1 9.7 %copy-start.1 = (bf16[512,512]{1,0:T(8,128)(2,1)S(1)}, bf16[512,512]{1,0:T(8,128)(2,1)}, u32[]{:S(2)}) copy-start(bf16[512,512]{1,0:T(8,128)(2,1)} %param.11) | copy-start | bytes 1572868
  153.1 37.5 %all-to-all-start = ((bf16[16,272,128]{2,1,0:T(8,128)(2,1)}), bf16[16,272,128]{2,1,0:T(8,128)(2,1)}, u32[]{:S(2)}, u32[]{:S(2)}) async-start(bf16[16,272,128]{2,1,0:T(8,128)(2,1)} %bitcast.30), calls=%async_computation | async-start | bytes 2228224 | tf_op jit(solution)/shard_map/all_to_all | solution.py:539
  162.8 3.0 %copy-start.12 = (s32[8]{0:T(128)S(1)}, s32[8]{0:T(128)}, u32[]{:S(2)}) copy-start(s32[8]{0:T(128)} %param.21) | copy-start | bytes 100
  162.8 3.1 %copy-start.6 = (bf16[8,64,64]{2,1,0:T(8,128)(2,1)S(1)}, bf16[8,64,64]{2,1,0:T(8,128)(2,1)}, u32[]{:S(2)}) copy-start(bf16[8,64,64]{2,1,0:T(8,128)(2,1)} %get-tuple-element.40) | copy-start | bytes 196612
  162.8 4.0 %copy-start.13 = (s32[8]{0:T(128)S(1)}, s32[8]{0:T(128)}, u32[]{:S(2)}) copy-start(s32[8]{0:T(128)} %param.20) | copy-start | bytes 100
  200.3 2.9 %copy-start.4 = (f32[8,2,64,4]{2,3,1,0:T(4,128)S(1)}, f32[8,2,64,4]{2,3,1,0:T(4,128)}, u32[]{:S(2)}) copy-start(f32[8,2,64,4]{2,3,1,0:T(4,128)} %copy.138) | copy-start | bytes 49156
  200.3 2.9 %copy-start.5 = (f32[8,2,64,4]{2,3,1,0:T(4,128)S(1)}, f32[8,2,64,4]{2,3,1,0:T(4,128)}, u32[]{:S(2)}) copy-start(f32[8,2,64,4]{2,3,1,0:T(4,128)} %copy.148) | copy-start | bytes 49156
  205.7 1.3 copy-start.10
  207.1 14.3 %copy-start.9 = (pred[128]{0:T(512)(128)(4,1)S(1)}, pred[128]{0:T(512)(128)(4,1)}, u32[]{:S(2)}) copy-start(pred[128]{0:T(512)(128)(4,1)} %fusion.59) | copy-start | bytes 388

commit v5 on v3

--- a/solution.py
+++ b/solution.py
@@ -513,7 +513,10 @@
         local_reqs,
     )
     home_lens = lax.dynamic_slice_in_dim(cache_lens, first_request, local_reqs, 0)
-    arrived = dp_exchange(packed(queries.reshape(local_reqs, -1), send_index), 4)
+    sending = packed(queries.reshape(local_reqs, -1), send_index)
+    arrived = lax.all_to_all(
+        sending.reshape(sending.shape[0], -1, 128), "dp", split_axis=0, concat_axis=0, tiled=True
+    ).reshape(sending.shape)
     slot_queries = packed(arrived, recv_index).reshape(queries.shape)
     top_score, weight_sum, summed = cache_merged(slot_queries, k_cache, v_cache, home_lens)
     value_width = summed.shape[1]

time: 224 us -> 226 us (level)
  Pallas kernels: 128 us -> 94.4 us
  waiting for transfers between devices: 20 us -> 46.8 us
  starting transfers between devices: 8.13 us -> 15.5 us
    pallas_call x1 -> x0, Pallas kernels: 35.1 us -> none  [dp_exchange(): pl.pallas_call(dp_exchange_kernel, out_shape=jax.ShapeDtypeStruct(tiles.s...]
    all_to_all x0 -> x1, waiting for transfers between devices: none -> 26.7 us  [shards(): lax.all_to_all(sending.reshape(sending.shape[0], -1, 128), 'dp', split_ax...]
    all_to_all x0 -> x1, starting transfers between devices: none -> 9.96 us  [shards(): lax.all_to_all(sending.reshape(sending.shape[0], -1, 128), 'dp', split_ax...]
    all_to_all x1, starting transfers between devices: 8.13 us -> 5.57 us  [shards(): lax.all_to_all(outgoing.reshape(outgoing.shape[0], -1, 128), 'dp', split_...]
  transfers between devices with their start and end apart: 1 -> 2, of which waited for: 1 -> 2; matrix products, arithmetic and copies ran while one was open for 4% -> 5% of each run, Pallas kernels for 0% -> 0%
where the time goes in v5:
time: 226 us; the launch traced here: 224 us
  Pallas kernels  94.4 us (42%)
  waiting for transfers between devices  46.8 us (21%)
  local copies, waits for them, and re-layouts  38.6 us (17%)
  starting transfers between devices  15.5 us (7%)
  matrix products  14.2 us (6%)
  other arithmetic  13.4 us (6%)
    pallas_call x3, Pallas kernels, axis_sum(): pl.pallas_call(functools.partial(axis_sum_kernel, axis, gather), out_shap...  55.7 us
    all_to_all x1, waiting for transfers between devices, shards(): lax.all_to_all(sending.reshape(sending.shape[0], -1, 128), 'dp', split_ax...  26.7 us
    all_to_all x1, waiting for transfers between devices, shards(): lax.all_to_all(outgoing.reshape(outgoing.shape[0], -1, 128), 'dp', split_...  20 us
    pallas_call x1, Pallas kernels, cache_merged(): pl.pallas_call(cache_kernel, grid_spec=pltpu.PrefetchScalarGridSpec(num_s...  18 us
    pallas_call x1, Pallas kernels, axis_gather(): pl.pallas_call(functools.partial(axis_gather_kernel, axis), out_shape=jax...  15 us
    all_to_all x1, starting transfers between devices, shards(): lax.all_to_all(sending.reshape(sending.shape[0], -1, 128), 'dp', split_ax...  9.96 us
    reshape x2, local copies, waits for them, and re-layouts, shards(): cache_values = back[:, :value_width].reshape(local_reqs, tree_slots, GROU...  8.24 us
    pallas_call x1, Pallas kernels, ty_max(): pl.pallas_call(ty_max_kernel, out_shape=jax.ShapeDtypeStruct(flat.shape,...  5.65 us
  transfers between devices with their start and end apart: 2, of which 2 were waited for; matrix products, arithmetic and copies ran while one was open for 5% of the time, Pallas kernels for 0%

profile of v5, /device:TPU:1, one launch (start us, length us, event | category | flops | bytes accessed | tf_op | source)
XLA Modules:
  0.0 224.2 jit_solution(6733498008847628829)
XLA Ops:
  0.7 1.3 multiply_reduce_fusion
  2.7 1.6 fusion.24
  4.5 1.3 reshape.307.x_ref
  5.8 24.3 %shard_map.122 = f32[816,128]{1,0:T(8,128)} custom-call(f32[3264,128]{1,0:T(8,128)} %reshape.307.x_ref), custom_call_target="tpu_custom_call" | custom-call | tf_op jit(solution)/shard_map/pallas_call | solution.py:275
  31.1 1.1 reshape.308
  40.7 15.0 %shard_map.123 = bf16[3072,128]{1,0:T(8,128)(2,1)} custom-call(bf16[768,128]{1,0:T(8,128)(2,1)} %reshape.309.x_ref), custom_call_target="tpu_custom_call" | custom-call | tf_op jit(solution)/shard_map/pallas_call | solution.py:379
  55.8 1.8 reshape.310
  58.4 1.2 copy.165
  59.6 10.0 %all-to-all-start = ((bf16[16,256,128]{2,1,0:T(8,128)(2,1)}), bf16[16,256,128]{2,1,0:T(8,128)(2,1)S(1)}, u32[]{:S(2)}, u32[]{:S(2)}) async-start(bf16[16,256,128]{2,1,0:T(8,128)(2,1)} %bitcast.26), calls=%async_computation | async-start | bytes 2097152 | tf_op jit(solution)/shard_map/all_to_all | solution.py:517
  70.7 26.7 %all-to-all-done = bf16[16,256,128]{2,1,0:T(8,128)(2,1)S(1)} async-done(((bf16[16,256,128]{2,1,0:T(8,128)(2,1)}), bf16[16,256,128]{2,1,0:T(8,128)(2,1)S(1)}, u32[]{:S(2)}, u32[]{:S(2)}) %all-to-all-start) | async-done | bytes 1048608 | tf_op jit(solution)/shard_map/all_to_all | solution.py:517
  97.5 1.5 convolution_convert_fusion.3
  98.9 2.0 reshape.313
  101.0 1.1 copy.190
  102.1 1.3 reshape.314.q_ref
  103.4 18.0 %shard_map.124 = (f32[8,2,256]{2,1,0:T(2,128)}, f32[8,2,256]{2,1,0:T(2,128)}, f32[8,256,128]{2,1,0:T(8,128)}) custom-call(s32[8]{0:T(128)} %dynamic_slice.28.lens_ref, s32[1]{0:T(128)} %bitcast.start_ref, bf16[8,256,128]{2,1,0:T(8,128)(2,1)} %reshape.314.q_ref, bf16[8,2048,128]{2,1,0:T(8,128)(2,1)} %k_ref.1, bf16[8,2048,128]{2,1,0:T(8,128)(2,1)} %v_ref.1), custom_call_target="tpu_custom_call" | custom-call | flops 4294967296 | bytes 9961472 | tf_op jit(solution)/shard_map/pallas_call | solution.py:136
  121.4 1.3 reshape.315.x_ref
  122.7 5.6 %shard_map.125 = f32[32,128]{1,0:T(8,128)} custom-call(f32[32,128]{1,0:T(8,128)} %reshape.315.x_ref), custom_call_target="tpu_custom_call" | custom-call | tf_op jit(solution)/shard_map/pallas_call | solution.py:396
  130.3 1.3 multiply_convert_fusion
  132.5 19.6 %shard_map.126 = bf16[2112,128]{1,0:T(8,128)(2,1)} custom-call(bf16[2112,128]{1,0:T(8,128)(2,1)} %fusion.23.x_ref), custom_call_target="tpu_custom_call" | custom-call | tf_op jit(solution)/shard_map/pallas_call | solution.py:275
  154.1 1.2 copy.167
  155.3 5.6 %all-to-all-start.1 = ((bf16[16,272,128]{2,1,0:T(8,128)(2,1)}), bf16[16,272,128]{2,1,0:T(8,128)(2,1)}, u32[]{:S(2)}, u32[]{:S(2)}) async-start(bf16[16,272,128]{2,1,0:T(8,128)(2,1)} %bitcast.30), calls=%async_computation.1 | async-start | bytes 2228224 | tf_op jit(solution)/shard_map/all_to_all | solution.py:540
  160.9 1.5 reshape.342
  162.4 1.1 convert_element_type.91
  167.1 2.4 %fusion.4 = (f32[8,64,2,4]{1,3,2,0:T(4,128)S(1)}, f32[8,2,64,64,4]{3,2,4,1,0:T(8,128)S(1)}) fusion(pred[8,64,64]{1,2,0:T(8,128)(4,1)S(1)} %copy.135, bf16[8,64,2,4,64]{4,3,2,1,0:T(4,128)(2,1)} %reshape.342, bf16[8,64,2,64,1]{1,0,3,2,4:T(8,128)(2,1)S(1)} %bitcast.104), kind=kOutput, calls=%fused_computation.12 | convolution fusion | flops 34336768 | bytes 1753088 | tf_op jit(solution)/shard_map/rtkgd,rukd->rtkgu/dot_general | solution.py:84
  170.2 20.0 %all-to-all-done.1 = bf16[16,272,128]{2,1,0:T(8,128)(2,1)} async-done(((bf16[16,272,128]{2,1,0:T(8,128)(2,1)}), bf16[16,272,128]{2,1,0:T(8,128)(2,1)}, u32[]{:S(2)}, u32[]{:S(2)}) %all-to-all-start.1) | async-done | bytes 1114144 | tf_op jit(solution)/shard_map/all_to_all | solution.py:540
  190.3 1.6 fusion
  196.0 4.1 %reshape.324 = f32[8,64,4,2,64]{4,3,2,1,0:T(2,128)} reshape(f32[8,32768]{1,0:T(8,128)} %slice.91) | data formatting | bytes 2097152 | tf_op jit(solution)/shard_map/reshape | solution.py:547
  200.1 4.1 %copy.132 = f32[8,64,4,2,64]{1,4,2,3,0:T(8,128)} copy(f32[8,64,4,2,64]{4,3,2,1,0:T(2,128)} %reshape.324) | data formatting | bytes 2097152 | tf_op jit(solution)/shard_map/reshape | solution.py:547
  204.3 2.5 %fusion.3 = bf16[8,64,2,4,64]{1,4,3,2,0:T(8,128)(2,1)S(1)} fusion(f32[8,64,4,2,64]{1,4,2,3,0:T(8,128)} %copy.132, f32[8,2,64,64,4]{3,2,4,1,0:T(8,128)S(1)} %get-tuple-element.42, f32[8,64,2,4]{1,3,2,0:T(4,128)S(1)} %get-tuple-element.22, f32[8,64,2,4]{1,3,2,0:T(4,128)S(1)} %get-tuple-element.23, f32[8,64,2,4]{1,3,2,0:T(4,128)S(1)} %get-tuple-element.41, ...), kind=kOutput, calls=%fused_computation.8 | convolution fusion | flops 36175872 | bytes 2850816 | tf_op jit(solution)/shard_map/rtkgu,rukd->rtkgd/dot_general | solution.py:91
  208.6 1.1 convert_element_type.111.x_ref
  209.7 11.8 %shard_map.127 = f32[512,128]{1,0:T(8,128)} custom-call(bf16[2048,128]{1,0:T(8,128)(2,1)} %convert_element_type.111.x_ref), custom_call_target="tpu_custom_call" | custom-call | tf_op jit(solution)/shard_map/pallas_call | solution.py:275
  222.5 1.7 select_convert_fusion
  (126 shorter events, 28.1 us)
Async XLA Ops:
  0.6 2.1 copy-start
  32.2 1.2 copy-start.8
  32.2 1.9 copy-start.7
  34.2 3.4 %copy-start.11 = (s32[128]{0:T(128)S(1)}, s32[128]{0:T(128)}, u32[]{:S(2)}) copy-start(s32[128]{0:T(128)} %param.17) | copy-start | bytes 1540
  57.6 2.0 copy-start.2
  59.6 37.9 %all-to-all-start = ((bf16[16,256,128]{2,1,0:T(8,128)(2,1)}), bf16[16,256,128]{2,1,0:T(8,128)(2,1)S(1)}, u32[]{:S(2)}, u32[]{:S(2)}) async-start(bf16[16,256,128]{2,1,0:T(8,128)(2,1)} %bitcast.26), calls=%async_computation | async-start | bytes 2097152 | tf_op jit(solution)/shard_map/all_to_all | solution.py:517
  131.7 21.5 %copy-start.3 = (f32[32,128]{1,0:T(8,128)S(1)}, f32[32,128]{1,0:T(8,128)}, u32[]{:S(2)}) copy-start(f32[32,128]{1,0:T(8,128)} %shard_map.125) | copy-start | bytes 49156
  152.1 1.4 slice-start
  155.3 7.1 %copy-start.1 = (bf16[512,512]{1,0:T(8,128)(2,1)S(1)}, bf16[512,512]{1,0:T(8,128)(2,1)}, u32[]{:S(2)}) copy-start(bf16[512,512]{1,0:T(8,128)(2,1)} %param.11) | copy-start | bytes 1572868
  155.3 35.0 %all-to-all-start.1 = ((bf16[16,272,128]{2,1,0:T(8,128)(2,1)}), bf16[16,272,128]{2,1,0:T(8,128)(2,1)}, u32[]{:S(2)}, u32[]{:S(2)}) async-start(bf16[16,272,128]{2,1,0:T(8,128)(2,1)} %bitcast.30), calls=%async_computation.1 | async-start | bytes 2228224 | tf_op jit(solution)/shard_map/all_to_all | solution.py:540
  162.4 3.0 %copy-start.12 = (s32[8]{0:T(128)S(1)}, s32[8]{0:T(128)}, u32[]{:S(2)}) copy-start(s32[8]{0:T(128)} %param.21) | copy-start | bytes 100
  162.4 3.1 %copy-start.6 = (bf16[8,64,64]{2,1,0:T(8,128)(2,1)S(1)}, bf16[8,64,64]{2,1,0:T(8,128)(2,1)}, u32[]{:S(2)}) copy-start(bf16[8,64,64]{2,1,0:T(8,128)(2,1)} %get-tuple-element.40) | copy-start | bytes 196612
  162.4 4.0 %copy-start.13 = (s32[8]{0:T(128)S(1)}, s32[8]{0:T(128)}, u32[]{:S(2)}) copy-start(s32[8]{0:T(128)} %param.20) | copy-start | bytes 100
  200.1 4.2 %copy-start.4 = (f32[8,2,64,4]{2,3,1,0:T(4,128)S(1)}, f32[8,2,64,4]{2,3,1,0:T(4,128)}, u32[]{:S(2)}) copy-start(f32[8,2,64,4]{2,3,1,0:T(4,128)} %copy.134) | copy-start | bytes 49156
  200.1 4.2 %copy-start.5 = (f32[8,2,64,4]{2,3,1,0:T(4,128)S(1)}, f32[8,2,64,4]{2,3,1,0:T(4,128)}, u32[]{:S(2)}) copy-start(f32[8,2,64,4]{2,3,1,0:T(4,128)} %copy.143) | copy-start | bytes 49156
  206.7 1.3 copy-start.10
  208.1 14.4 %copy-start.9 = (pred[128]{0:T(512)(128)(4,1)S(1)}, pred[128]{0:T(512)(128)(4,1)}, u32[]{:S(2)}) copy-start(pred[128]{0:T(512)(128)(4,1)} %fusion.59) | copy-start | bytes 388

commit v6 on v3

--- a/solution.py
+++ b/solution.py
@@ -265,6 +265,62 @@
         out_ref[pl.ds(pl.multiple_of(source * chunk, 16), chunk)] = gathered[step - 1]
 
 
+def relay_sum_kernel(axis, x_ref, out_ref, held, halves, forwarded, sems):
+    n = lax.axis_size(axis)
+    me = lax.axis_index(axis)
+    chunk = held.shape[1]
+    half = chunk // 2
+    where = {name: lax.axis_index(name) for name in ("dp", "tx", "ty")}
+
+    def device(peer):
+        return tuple(peer if name == axis else where[name] for name in ("dp", "tx", "ty"))
+
+    right = lax.rem(me + 1, n)
+    left = lax.rem(me + n - 1, n)
+    across = lax.rem(me + 2, n)
+
+    def rows(index, start, size):
+        return pl.ds(pl.multiple_of(index * chunk + start, 8), size)
+
+    def remote(src, dst, slot, peer):
+        return pltpu.make_async_remote_copy(
+            src_ref=src,
+            dst_ref=dst,
+            send_sem=sems.at[0, slot],
+            recv_sem=sems.at[1, slot],
+            device_id=device(peer),
+            device_id_type=pl.DeviceIdType.MESH,
+        )
+
+    barrier = pltpu.get_barrier_semaphore()
+    for peer in (left, right):
+        pl.semaphore_signal(barrier, inc=1, device_id=device(peer), device_id_type=pl.DeviceIdType.MESH)
+    pl.semaphore_wait(barrier, 2)
+    direct_right = remote(x_ref.at[rows(right, 0, chunk)], held.at[0], 0, right)
+    direct_left = remote(x_ref.at[rows(left, 0, chunk)], held.at[1], 1, left)
+    relay_right = remote(x_ref.at[rows(across, 0, half)], halves.at[0], 2, right)
+    relay_left = remote(x_ref.at[rows(across, half, half)], halves.at[1], 3, left)
+    for copy in (direct_right, direct_left, relay_right, relay_left):
+        copy.start()
+    relay_right.wait()
+    onward_right = remote(halves.at[0], forwarded.at[0], 4, right)
+    onward_right.start()
+    relay_left.wait()
+    onward_left = remote(halves.at[1], forwarded.at[1], 5, left)
+    onward_left.start()
+    for copy in (direct_right, direct_left, onward_right, onward_left):
+        copy.wait()
+    for part in range(2):
+        mine = x_ref[rows(me, part * half, half)].astype(jnp.float32)
+        total = (
+            mine
+            + held[0, pl.ds(part * half, half)].astype(jnp.float32)
+            + held[1, pl.ds(part * half, half)].astype(jnp.float32)
+            + forwarded[part].astype(jnp.float32)
+        )
+        out_ref[pl.ds(part * half, half)] = total.astype(out_ref.dtype)
+
+
 def axis_sum(values, axis, gather, send_type, out_type, collective_id):
     n = lax.axis_size(axis)
     flat = values.reshape(-1, 128).astype(send_type)
@@ -272,6 +328,20 @@
     padded = -(-rows // (16 * n)) * 16 * n
     flat = jnp.pad(flat, ((0, padded - rows), (0, 0)))
     chunk = padded // n
+    if not gather and n == 4:
+        return pl.pallas_call(
+            functools.partial(relay_sum_kernel, axis),
+            out_shape=jax.ShapeDtypeStruct((chunk, 128), out_type),
+            in_specs=[pl.BlockSpec(memory_space=pltpu.VMEM)],
+            out_specs=pl.BlockSpec(memory_space=pltpu.VMEM),
+            scratch_shapes=[
+                pltpu.VMEM((2, chunk, 128), send_type),
+                pltpu.VMEM((2, chunk // 2, 128), send_type),
+                pltpu.VMEM((2, chunk // 2, 128), send_type),
+                pltpu.SemaphoreType.DMA((2, 6)),
+            ],
+            compiler_params=pltpu.CompilerParams(collective_id=collective_id, has_side_effects=True),
+        )(flat)
     out = pl.pallas_call(
         functools.partial(axis_sum_kernel, axis, gather),
         out_shape=jax.ShapeDtypeStruct((padded if gather else chunk, 128), out_type),

time: 224 us -> 225 us (level)
  Pallas kernels: 128 us -> 131 us
    pallas_call x0 -> x2, Pallas kernels: none -> 37.8 us  [axis_sum(): pl.pallas_call(functools.partial(relay_sum_kernel, axis), out_shape=jax.S...]
    pallas_call x3 -> x1, Pallas kernels: 53.8 us -> 20.2 us  [axis_sum(): pl.pallas_call(functools.partial(axis_sum_kernel, axis, gather), out_shap...]
    pallas_call x1, Pallas kernels: 15 us -> 11.3 us  [axis_gather(): pl.pallas_call(functools.partial(axis_gather_kernel, axis), out_shape=jax...]
    pallas_call x1, Pallas kernels: 35.1 us -> 37.4 us  [dp_exchange(): pl.pallas_call(dp_exchange_kernel, out_shape=jax.ShapeDtypeStruct(tiles.s...]
where the time goes in v6:
time: 225 us; the launch traced here: 224 us
  Pallas kernels  131 us (58%)
  local copies, waits for them, and re-layouts  37.8 us (17%)
  waiting for transfers between devices  20 us (9%)
  matrix products  14.7 us (7%)
  other arithmetic  13.4 us (6%)
  starting transfers between devices  6.4 us (3%)
    pallas_call x2, Pallas kernels, axis_sum(): pl.pallas_call(functools.partial(relay_sum_kernel, axis), out_shape=jax.S...  37.8 us
    pallas_call x1, Pallas kernels, dp_exchange(): pl.pallas_call(dp_exchange_kernel, out_shape=jax.ShapeDtypeStruct(tiles.s...  37.4 us
    pallas_call x1, Pallas kernels, axis_sum(): pl.pallas_call(functools.partial(axis_sum_kernel, axis, gather), out_shap...  20.2 us
    all_to_all x1, waiting for transfers between devices, shards(): lax.all_to_all(outgoing.reshape(outgoing.shape[0], -1, 128), 'dp', split_...  20 us
    pallas_call x1, Pallas kernels, cache_merged(): pl.pallas_call(cache_kernel, grid_spec=pltpu.PrefetchScalarGridSpec(num_s...  18.1 us
    pallas_call x1, Pallas kernels, axis_gather(): pl.pallas_call(functools.partial(axis_gather_kernel, axis), out_shape=jax...  11.3 us
    reshape x2, local copies, waits for them, and re-layouts, shards(): cache_values = back[:, :value_width].reshape(local_reqs, tree_slots, GROU...  8.24 us
    all_to_all x1, starting transfers between devices, shards(): lax.all_to_all(outgoing.reshape(outgoing.shape[0], -1, 128), 'dp', split_...  6.4 us
  transfers between devices with their start and end apart: 1, of which 1 were waited for; matrix products, arithmetic and copies ran while one was open for 4% of the time, Pallas kernels for 0%

profile of v6, /device:TPU:1, one launch (start us, length us, event | category | flops | bytes accessed | tf_op | source)
XLA Modules:
  0.0 224.1 jit_solution(371473322245512844)
XLA Ops:
  0.7 1.3 multiply_reduce_fusion
  2.7 1.6 fusion.24
  4.5 1.3 reshape.307.x_ref
  5.8 24.5 %shard_map.122 = f32[816,128]{1,0:T(8,128)} custom-call(f32[3264,128]{1,0:T(8,128)} %reshape.307.x_ref), custom_call_target="tpu_custom_call" | custom-call | tf_op jit(solution)/shard_map/pallas_call | solution.py:332
  31.3 1.1 reshape.308
  36.5 1.1 fusion.37
  41.6 11.3 %shard_map.123 = bf16[3072,128]{1,0:T(8,128)(2,1)} custom-call(bf16[768,128]{1,0:T(8,128)(2,1)} %reshape.309.x_ref), custom_call_target="tpu_custom_call" | custom-call | tf_op jit(solution)/shard_map/pallas_call | solution.py:449
  52.9 2.0 reshape.310
  55.7 1.2 copy.165
  56.9 37.4 %shard_map.124 = bf16[16,256,128]{2,1,0:T(8,128)(2,1)} custom-call(bf16[16,256,128]{2,1,0:T(8,128)(2,1)} %bitcast.98), custom_call_target="tpu_custom_call" | custom-call | tf_op jit(solution)/shard_map/pallas_call | solution.py:395
  94.6 1.9 convolution_convert_fusion.3
  96.5 1.1 reshape.313
  98.7 1.3 reshape.314.q_ref
  100.0 18.1 %shard_map.125 = (f32[8,2,256]{2,1,0:T(2,128)}, f32[8,2,256]{2,1,0:T(2,128)}, f32[8,256,128]{2,1,0:T(8,128)}) custom-call(s32[8]{0:T(128)} %dynamic_slice.28.lens_ref, s32[1]{0:T(128)} %bitcast.start_ref, bf16[8,256,128]{2,1,0:T(8,128)(2,1)} %reshape.314.q_ref, bf16[8,2048,128]{2,1,0:T(8,128)(2,1)} %k_ref.1, bf16[8,2048,128]{2,1,0:T(8,128)(2,1)} %v_ref.1), custom_call_target="tpu_custom_call" | custom-call | flops 4294967296 | bytes 9961472 | tf_op jit(solution)/shard_map/pallas_call | solution.py:136
  118.1 1.3 reshape.315.x_ref
  119.4 5.8 %shard_map.126 = f32[32,128]{1,0:T(8,128)} custom-call(f32[32,128]{1,0:T(8,128)} %reshape.315.x_ref), custom_call_target="tpu_custom_call" | custom-call | tf_op jit(solution)/shard_map/pallas_call | solution.py:466
  127.1 1.3 multiply_convert_fusion
  129.3 20.2 %shard_map.127 = bf16[2112,128]{1,0:T(8,128)(2,1)} custom-call(bf16[2112,128]{1,0:T(8,128)(2,1)} %fusion.23.x_ref), custom_call_target="tpu_custom_call" | custom-call | tf_op jit(solution)/shard_map/pallas_call | solution.py:345
  149.6 1.1 slice.74
  151.7 1.2 copy.167
  152.9 6.4 %all-to-all-start = ((bf16[16,272,128]{2,1,0:T(8,128)(2,1)}), bf16[16,272,128]{2,1,0:T(8,128)(2,1)}, u32[]{:S(2)}, u32[]{:S(2)}) async-start(bf16[16,272,128]{2,1,0:T(8,128)(2,1)} %bitcast.30), calls=%async_computation | async-start | bytes 2228224 | tf_op jit(solution)/shard_map/all_to_all | solution.py:607
  159.3 1.5 reshape.342
  160.9 1.1 convert_element_type.91
  165.5 2.4 %fusion.4 = (f32[8,64,2,4]{1,3,2,0:T(4,128)S(1)}, f32[8,2,64,64,4]{3,2,4,1,0:T(8,128)S(1)}) fusion(pred[8,64,64]{1,2,0:T(8,128)(4,1)S(1)} %copy.135, bf16[8,64,2,4,64]{4,3,2,1,0:T(4,128)(2,1)} %reshape.342, bf16[8,64,2,64,1]{1,0,3,2,4:T(8,128)(2,1)S(1)} %bitcast.105), kind=kOutput, calls=%fused_computation.12 | convolution fusion | flops 34336768 | bytes 1753088 | tf_op jit(solution)/shard_map/rtkgd,rukd->rtkgu/dot_general | solution.py:84
  168.7 20.0 %all-to-all-done = bf16[16,272,128]{2,1,0:T(8,128)(2,1)} async-done(((bf16[16,272,128]{2,1,0:T(8,128)(2,1)}), bf16[16,272,128]{2,1,0:T(8,128)(2,1)}, u32[]{:S(2)}, u32[]{:S(2)}) %all-to-all-start) | async-done | bytes 1114144 | tf_op jit(solution)/shard_map/all_to_all | solution.py:607
  188.7 1.6 fusion
  194.4 4.1 %reshape.324 = f32[8,64,4,2,64]{4,3,2,1,0:T(2,128)} reshape(f32[8,32768]{1,0:T(8,128)} %slice.91) | data formatting | bytes 2097152 | tf_op jit(solution)/shard_map/reshape | solution.py:614
  198.5 4.1 %copy.132 = f32[8,64,4,2,64]{1,4,2,3,0:T(8,128)} copy(f32[8,64,4,2,64]{4,3,2,1,0:T(2,128)} %reshape.324) | data formatting | bytes 2097152 | tf_op jit(solution)/shard_map/reshape | solution.py:614
  202.7 2.5 %fusion.3 = bf16[8,64,2,4,64]{1,4,3,2,0:T(8,128)(2,1)S(1)} fusion(f32[8,64,4,2,64]{1,4,2,3,0:T(8,128)} %copy.132, f32[8,2,64,64,4]{3,2,4,1,0:T(8,128)S(1)} %get-tuple-element.42, f32[8,64,2,4]{1,3,2,0:T(4,128)S(1)} %get-tuple-element.22, f32[8,64,2,4]{1,3,2,0:T(4,128)S(1)} %get-tuple-element.23, f32[8,64,2,4]{1,3,2,0:T(4,128)S(1)} %get-tuple-element.41, ...), kind=kOutput, calls=%fused_computation.8 | convolution fusion | flops 36175872 | bytes 2850816 | tf_op jit(solution)/shard_map/rtkgu,rukd->rtkgd/dot_general | solution.py:91
  207.0 1.1 convert_element_type.111.x_ref
  208.1 13.4 %shard_map.128 = f32[512,128]{1,0:T(8,128)} custom-call(bf16[2048,128]{1,0:T(8,128)(2,1)} %convert_element_type.111.x_ref), custom_call_target="tpu_custom_call" | custom-call | tf_op jit(solution)/shard_map/pallas_call | solution.py:332
  222.4 1.7 select_convert_fusion
  (125 shorter events, 26.9 us)
Async XLA Ops:
  0.6 2.1 copy-start
  32.4 1.2 copy-start.8
  32.4 2.0 copy-start.7
  34.4 3.4 %copy-start.11 = (s32[128]{0:T(128)S(1)}, s32[128]{0:T(128)}, u32[]{:S(2)}) copy-start(s32[128]{0:T(128)} %param.17) | copy-start | bytes 1540
  54.9 2.0 copy-start.2
  128.4 22.2 %copy-start.3 = (f32[32,128]{1,0:T(8,128)S(1)}, f32[32,128]{1,0:T(8,128)}, u32[]{:S(2)}) copy-start(f32[32,128]{1,0:T(8,128)} %shard_map.126) | copy-start | bytes 49156
  149.5 1.6 slice-start
  152.9 7.9 %copy-start.1 = (bf16[512,512]{1,0:T(8,128)(2,1)S(1)}, bf16[512,512]{1,0:T(8,128)(2,1)}, u32[]{:S(2)}) copy-start(bf16[512,512]{1,0:T(8,128)(2,1)} %param.11) | copy-start | bytes 1572868
  152.9 35.8 %all-to-all-start = ((bf16[16,272,128]{2,1,0:T(8,128)(2,1)}), bf16[16,272,128]{2,1,0:T(8,128)(2,1)}, u32[]{:S(2)}, u32[]{:S(2)}) async-start(bf16[16,272,128]{2,1,0:T(8,128)(2,1)} %bitcast.30), calls=%async_computation | async-start | bytes 2228224 | tf_op jit(solution)/shard_map/all_to_all | solution.py:607
  160.8 3.0 %copy-start.12 = (s32[8]{0:T(128)S(1)}, s32[8]{0:T(128)}, u32[]{:S(2)}) copy-start(s32[8]{0:T(128)} %param.21) | copy-start | bytes 100
  160.8 3.1 %copy-start.6 = (bf16[8,64,64]{2,1,0:T(8,128)(2,1)S(1)}, bf16[8,64,64]{2,1,0:T(8,128)(2,1)}, u32[]{:S(2)}) copy-start(bf16[8,64,64]{2,1,0:T(8,128)(2,1)} %get-tuple-element.40) | copy-start | bytes 196612
  160.8 4.0 %copy-start.13 = (s32[8]{0:T(128)S(1)}, s32[8]{0:T(128)}, u32[]{:S(2)}) copy-start(s32[8]{0:T(128)} %param.20) | copy-start | bytes 100
  198.5 4.2 %copy-start.4 = (f32[8,2,64,4]{2,3,1,0:T(4,128)S(1)}, f32[8,2,64,4]{2,3,1,0:T(4,128)}, u32[]{:S(2)}) copy-start(f32[8,2,64,4]{2,3,1,0:T(4,128)} %copy.134) | copy-start | bytes 49156
  198.5 4.2 %copy-start.5 = (f32[8,2,64,4]{2,3,1,0:T(4,128)S(1)}, f32[8,2,64,4]{2,3,1,0:T(4,128)}, u32[]{:S(2)}) copy-start(f32[8,2,64,4]{2,3,1,0:T(4,128)} %copy.143) | copy-start | bytes 49156
  205.1 1.3 copy-start.10
  206.5 16.0 %copy-start.9 = (pred[128]{0:T(512)(128)(4,1)S(1)}, pred[128]{0:T(512)(128)(4,1)}, u32[]{:S(2)}) copy-start(pred[128]{0:T(512)(128)(4,1)} %fusion.59) | copy-start | bytes 388

commit v7 on v3

--- a/solution.py
+++ b/solution.py
@@ -303,7 +303,7 @@
         peer = lax.rem(me + step, n)
         copy = pltpu.make_async_remote_copy(
             src_ref=x_ref.at[peer],
-            dst_ref=held.at[step - 1],
+            dst_ref=out_ref.at[me],
             send_sem=sems.at[0, step - 1],
             recv_sem=sems.at[1, step - 1],
             device_id=(peer, col, row),
@@ -314,8 +314,6 @@
     out_ref[me] = x_ref[me]
     for copy in copies:
         copy.wait()
-    for step in range(1, n):
-        out_ref[lax.rem(me - step + n, n)] = held[step - 1]
 
 
 def dp_exchange(blocks, collective_id):

time: 224 us -> 224 us (level)
  no operation moved by 1% of the time
where the time goes in v7:
time: 224 us; the launch traced here: 223 us
  Pallas kernels  128 us (57%)
  local copies, waits for them, and re-layouts  37.8 us (17%)
  waiting for transfers between devices  20 us (9%)
  matrix products  14.7 us (7%)
  other arithmetic  13.4 us (6%)
  starting transfers between devices  8.03 us (4%)
    pallas_call x3, Pallas kernels, axis_sum(): pl.pallas_call(functools.partial(axis_sum_kernel, axis, gather), out_shap...  53.9 us
    pallas_call x1, Pallas kernels, dp_exchange(): pl.pallas_call(dp_exchange_kernel, out_shape=jax.ShapeDtypeStruct(tiles.s...  35 us
    all_to_all x1, waiting for transfers between devices, shards(): lax.all_to_all(outgoing.reshape(outgoing.shape[0], -1, 128), 'dp', split_...  20 us
    pallas_call x1, Pallas kernels, cache_merged(): pl.pallas_call(cache_kernel, grid_spec=pltpu.PrefetchScalarGridSpec(num_s...  18.1 us
    pallas_call x1, Pallas kernels, axis_gather(): pl.pallas_call(functools.partial(axis_gather_kernel, axis), out_shape=jax...  15 us
    reshape x2, local copies, waits for them, and re-layouts, shards(): cache_values = back[:, :value_width].reshape(local_reqs, tree_slots, GROU...  8.24 us
    all_to_all x1, starting transfers between devices, shards(): lax.all_to_all(outgoing.reshape(outgoing.shape[0], -1, 128), 'dp', split_...  8.03 us
    pallas_call x1, Pallas kernels, ty_max(): pl.pallas_call(ty_max_kernel, out_shape=jax.ShapeDtypeStruct(flat.shape,...  5.78 us
  transfers between devices with their start and end apart: 1, of which 1 were waited for; matrix products, arithmetic and copies ran while one was open for 4% of the time, Pallas kernels for 0%

profile of v7, /device:TPU:1, one launch (start us, length us, event | category | flops | bytes accessed | tf_op | source)
XLA Modules:
  0.0 223.0 jit_solution(15124056457390199905)
XLA Ops:
  0.7 1.3 multiply_reduce_fusion
  2.7 1.6 fusion.24
  4.5 1.3 reshape.307.x_ref
  5.8 24.3 %shard_map.122 = f32[816,128]{1,0:T(8,128)} custom-call(f32[3264,128]{1,0:T(8,128)} %reshape.307.x_ref), custom_call_target="tpu_custom_call" | custom-call | tf_op jit(solution)/shard_map/pallas_call | solution.py:275
  31.1 1.1 reshape.308
  36.3 1.1 fusion.37
  41.4 15.0 %shard_map.123 = bf16[3072,128]{1,0:T(8,128)(2,1)} custom-call(bf16[768,128]{1,0:T(8,128)(2,1)} %reshape.309.x_ref), custom_call_target="tpu_custom_call" | custom-call | tf_op jit(solution)/shard_map/pallas_call | solution.py:377
  56.5 2.0 reshape.310
  59.2 1.2 copy.165
  60.4 35.0 %shard_map.124 = bf16[16,256,128]{2,1,0:T(8,128)(2,1)} custom-call(bf16[16,256,128]{2,1,0:T(8,128)(2,1)} %bitcast.98), custom_call_target="tpu_custom_call" | custom-call | tf_op jit(solution)/shard_map/pallas_call | solution.py:323
  95.8 1.9 convolution_convert_fusion.3
  97.7 1.1 reshape.313
  99.9 1.3 reshape.314.q_ref
  101.2 18.1 %shard_map.125 = (f32[8,2,256]{2,1,0:T(2,128)}, f32[8,2,256]{2,1,0:T(2,128)}, f32[8,256,128]{2,1,0:T(8,128)}) custom-call(s32[8]{0:T(128)} %dynamic_slice.28.lens_ref, s32[1]{0:T(128)} %bitcast.start_ref, bf16[8,256,128]{2,1,0:T(8,128)(2,1)} %reshape.314.q_ref, bf16[8,2048,128]{2,1,0:T(8,128)(2,1)} %k_ref.1, bf16[8,2048,128]{2,1,0:T(8,128)(2,1)} %v_ref.1), custom_call_target="tpu_custom_call" | custom-call | flops 4294967296 | bytes 9961472 | tf_op jit(solution)/shard_map/pallas_call | solution.py:136
  119.3 1.3 reshape.315.x_ref
  120.6 5.8 %shard_map.126 = f32[32,128]{1,0:T(8,128)} custom-call(f32[32,128]{1,0:T(8,128)} %reshape.315.x_ref), custom_call_target="tpu_custom_call" | custom-call | tf_op jit(solution)/shard_map/pallas_call | solution.py:394
  128.3 1.3 multiply_convert_fusion
  130.5 17.8 %shard_map.127 = bf16[2112,128]{1,0:T(8,128)(2,1)} custom-call(bf16[2112,128]{1,0:T(8,128)(2,1)} %fusion.23.x_ref), custom_call_target="tpu_custom_call" | custom-call | tf_op jit(solution)/shard_map/pallas_call | solution.py:275
  148.3 1.1 slice.74
  150.5 1.2 copy.167
  151.7 8.0 %all-to-all-start = ((bf16[16,272,128]{2,1,0:T(8,128)(2,1)}), bf16[16,272,128]{2,1,0:T(8,128)(2,1)}, u32[]{:S(2)}, u32[]{:S(2)}) async-start(bf16[16,272,128]{2,1,0:T(8,128)(2,1)} %bitcast.30), calls=%async_computation | async-start | bytes 2228224 | tf_op jit(solution)/shard_map/all_to_all | solution.py:535
  159.7 1.5 reshape.342
  161.3 1.1 convert_element_type.91
  166.0 2.4 %fusion.4 = (f32[8,64,2,4]{1,3,2,0:T(4,128)S(1)}, f32[8,2,64,64,4]{3,2,4,1,0:T(8,128)S(1)}) fusion(pred[8,64,64]{1,2,0:T(8,128)(4,1)S(1)} %copy.135, bf16[8,64,2,4,64]{4,3,2,1,0:T(4,128)(2,1)} %reshape.342, bf16[8,64,2,64,1]{1,0,3,2,4:T(8,128)(2,1)S(1)} %bitcast.105), kind=kOutput, calls=%fused_computation.12 | convolution fusion | flops 34336768 | bytes 1753088 | tf_op jit(solution)/shard_map/rtkgd,rukd->rtkgu/dot_general | solution.py:84
  169.1 20.0 %all-to-all-done = bf16[16,272,128]{2,1,0:T(8,128)(2,1)} async-done(((bf16[16,272,128]{2,1,0:T(8,128)(2,1)}), bf16[16,272,128]{2,1,0:T(8,128)(2,1)}, u32[]{:S(2)}, u32[]{:S(2)}) %all-to-all-start) | async-done | bytes 1114144 | tf_op jit(solution)/shard_map/all_to_all | solution.py:535
  189.1 1.6 fusion
  194.8 4.1 %reshape.324 = f32[8,64,4,2,64]{4,3,2,1,0:T(2,128)} reshape(f32[8,32768]{1,0:T(8,128)} %slice.91) | data formatting | bytes 2097152 | tf_op jit(solution)/shard_map/reshape | solution.py:542
  198.9 4.1 %copy.132 = f32[8,64,4,2,64]{1,4,2,3,0:T(8,128)} copy(f32[8,64,4,2,64]{4,3,2,1,0:T(2,128)} %reshape.324) | data formatting | bytes 2097152 | tf_op jit(solution)/shard_map/reshape | solution.py:542
  203.1 2.5 %fusion.3 = bf16[8,64,2,4,64]{1,4,3,2,0:T(8,128)(2,1)S(1)} fusion(f32[8,64,4,2,64]{1,4,2,3,0:T(8,128)} %copy.132, f32[8,2,64,64,4]{3,2,4,1,0:T(8,128)S(1)} %get-tuple-element.42, f32[8,64,2,4]{1,3,2,0:T(4,128)S(1)} %get-tuple-element.22, f32[8,64,2,4]{1,3,2,0:T(4,128)S(1)} %get-tuple-element.23, f32[8,64,2,4]{1,3,2,0:T(4,128)S(1)} %get-tuple-element.41, ...), kind=kOutput, calls=%fused_computation.8 | convolution fusion | flops 36175872 | bytes 2850816 | tf_op jit(solution)/shard_map/rtkgu,rukd->rtkgd/dot_general | solution.py:91
  207.4 1.1 convert_element_type.111.x_ref
  208.5 11.8 %shard_map.128 = f32[512,128]{1,0:T(8,128)} custom-call(bf16[2048,128]{1,0:T(8,128)(2,1)} %convert_element_type.111.x_ref), custom_call_target="tpu_custom_call" | custom-call | tf_op jit(solution)/shard_map/pallas_call | solution.py:275
  221.3 1.7 select_convert_fusion
  (125 shorter events, 26.9 us)
Async XLA Ops:
  0.6 2.1 copy-start
  32.2 1.2 copy-start.8
  32.2 2.0 copy-start.7
  34.2 3.4 %copy-start.11 = (s32[128]{0:T(128)S(1)}, s32[128]{0:T(128)}, u32[]{:S(2)}) copy-start(s32[128]{0:T(128)} %param.17) | copy-start | bytes 1540
  58.4 2.0 copy-start.2
  129.6 19.8 %copy-start.3 = (f32[32,128]{1,0:T(8,128)S(1)}, f32[32,128]{1,0:T(8,128)}, u32[]{:S(2)}) copy-start(f32[32,128]{1,0:T(8,128)} %shard_map.126) | copy-start | bytes 49156
  148.3 1.6 slice-start
  151.7 9.6 %copy-start.1 = (bf16[512,512]{1,0:T(8,128)(2,1)S(1)}, bf16[512,512]{1,0:T(8,128)(2,1)}, u32[]{:S(2)}) copy-start(bf16[512,512]{1,0:T(8,128)(2,1)} %param.11) | copy-start | bytes 1572868
  151.7 37.4 %all-to-all-start = ((bf16[16,272,128]{2,1,0:T(8,128)(2,1)}), bf16[16,272,128]{2,1,0:T(8,128)(2,1)}, u32[]{:S(2)}, u32[]{:S(2)}) async-start(bf16[16,272,128]{2,1,0:T(8,128)(2,1)} %bitcast.30), calls=%async_computation | async-start | bytes 2228224 | tf_op jit(solution)/shard_map/all_to_all | solution.py:535
  161.3 3.0 %copy-start.12 = (s32[8]{0:T(128)S(1)}, s32[8]{0:T(128)}, u32[]{:S(2)}) copy-start(s32[8]{0:T(128)} %param.21) | copy-start | bytes 100
  161.3 3.1 %copy-start.6 = (bf16[8,64,64]{2,1,0:T(8,128)(2,1)S(1)}, bf16[8,64,64]{2,1,0:T(8,128)(2,1)}, u32[]{:S(2)}) copy-start(bf16[8,64,64]{2,1,0:T(8,128)(2,1)} %get-tuple-element.40) | copy-start | bytes 196612
  161.3 4.0 %copy-start.13 = (s32[8]{0:T(128)S(1)}, s32[8]{0:T(128)}, u32[]{:S(2)}) copy-start(s32[8]{0:T(128)} %param.20) | copy-start | bytes 100
  198.9 4.2 %copy-start.4 = (f32[8,2,64,4]{2,3,1,0:T(4,128)S(1)}, f32[8,2,64,4]{2,3,1,0:T(4,128)}, u32[]{:S(2)}) copy-start(f32[8,2,64,4]{2,3,1,0:T(4,128)} %copy.134) | copy-start | bytes 49156
  198.9 4.2 %copy-start.5 = (f32[8,2,64,4]{2,3,1,0:T(4,128)S(1)}, f32[8,2,64,4]{2,3,1,0:T(4,128)}, u32[]{:S(2)}) copy-start(f32[8,2,64,4]{2,3,1,0:T(4,128)} %copy.143) | copy-start | bytes 49156
  205.6 1.3 copy-start.10
  206.9 14.4 %copy-start.9 = (pred[128]{0:T(512)(128)(4,1)S(1)}, pred[128]{0:T(512)(128)(4,1)}, u32[]{:S(2)}) copy-start(pred[128]{0:T(512)(128)(4,1)} %fusion.59) | copy-start | bytes 388

commit v8 on v3

--- a/solution.py
+++ b/solution.py
@@ -312,9 +312,8 @@
         copy.start()
         copies.append(copy)
     out_ref[me] = x_ref[me]
-    for copy in copies:
+    for step, copy in enumerate(copies, start=1):
         copy.wait()
-    for step in range(1, n):
         out_ref[lax.rem(me - step + n, n)] = held[step - 1]
 
 

time: 224 us -> 224 us (level)
  no operation moved by 1% of the time
where the time goes in v8:
time: 224 us; the launch traced here: 223 us
  Pallas kernels  128 us (57%)
  local copies, waits for them, and re-layouts  37.8 us (17%)
  waiting for transfers between devices  20 us (9%)
  matrix products  14.7 us (7%)
  other arithmetic  13.4 us (6%)
  starting transfers between devices  8.05 us (4%)
    pallas_call x3, Pallas kernels, axis_sum(): pl.pallas_call(functools.partial(axis_sum_kernel, axis, gather), out_shap...  53.9 us
    pallas_call x1, Pallas kernels, dp_exchange(): pl.pallas_call(dp_exchange_kernel, out_shape=jax.ShapeDtypeStruct(tiles.s...  35 us
    all_to_all x1, waiting for transfers between devices, shards(): lax.all_to_all(outgoing.reshape(outgoing.shape[0], -1, 128), 'dp', split_...  20 us
    pallas_call x1, Pallas kernels, cache_merged(): pl.pallas_call(cache_kernel, grid_spec=pltpu.PrefetchScalarGridSpec(num_s...  18 us
    pallas_call x1, Pallas kernels, axis_gather(): pl.pallas_call(functools.partial(axis_gather_kernel, axis), out_shape=jax...  15 us
    reshape x2, local copies, waits for them, and re-layouts, shards(): cache_values = back[:, :value_width].reshape(local_reqs, tree_slots, GROU...  8.24 us
    all_to_all x1, starting transfers between devices, shards(): lax.all_to_all(outgoing.reshape(outgoing.shape[0], -1, 128), 'dp', split_...  8.05 us
    pallas_call x1, Pallas kernels, ty_max(): pl.pallas_call(ty_max_kernel, out_shape=jax.ShapeDtypeStruct(flat.shape,...  5.78 us
  transfers between devices with their start and end apart: 1, of which 1 were waited for; matrix products, arithmetic and copies ran while one was open for 4% of the time, Pallas kernels for 0%

profile of v8, /device:TPU:1, one launch (start us, length us, event | category | flops | bytes accessed | tf_op | source)
XLA Modules:
  0.0 223.0 jit_solution(7280939331122543506)
XLA Ops:
  0.7 1.3 multiply_reduce_fusion
  2.7 1.6 fusion.24
  4.5 1.3 reshape.307.x_ref
  5.8 24.3 %shard_map.122 = f32[816,128]{1,0:T(8,128)} custom-call(f32[3264,128]{1,0:T(8,128)} %reshape.307.x_ref), custom_call_target="tpu_custom_call" | custom-call | tf_op jit(solution)/shard_map/pallas_call | solution.py:275
  31.1 1.1 reshape.308
  36.3 1.1 fusion.37
  41.4 15.0 %shard_map.123 = bf16[3072,128]{1,0:T(8,128)(2,1)} custom-call(bf16[768,128]{1,0:T(8,128)(2,1)} %reshape.309.x_ref), custom_call_target="tpu_custom_call" | custom-call | tf_op jit(solution)/shard_map/pallas_call | solution.py:378
  56.5 2.0 reshape.310
  59.2 1.2 copy.165
  60.4 35.0 %shard_map.124 = bf16[16,256,128]{2,1,0:T(8,128)(2,1)} custom-call(bf16[16,256,128]{2,1,0:T(8,128)(2,1)} %bitcast.98), custom_call_target="tpu_custom_call" | custom-call | tf_op jit(solution)/shard_map/pallas_call | solution.py:324
  95.8 1.9 convolution_convert_fusion.3
  97.7 1.1 reshape.313
  99.9 1.3 reshape.314.q_ref
  101.2 18.0 %shard_map.125 = (f32[8,2,256]{2,1,0:T(2,128)}, f32[8,2,256]{2,1,0:T(2,128)}, f32[8,256,128]{2,1,0:T(8,128)}) custom-call(s32[8]{0:T(128)} %dynamic_slice.28.lens_ref, s32[1]{0:T(128)} %bitcast.start_ref, bf16[8,256,128]{2,1,0:T(8,128)(2,1)} %reshape.314.q_ref, bf16[8,2048,128]{2,1,0:T(8,128)(2,1)} %k_ref.1, bf16[8,2048,128]{2,1,0:T(8,128)(2,1)} %v_ref.1), custom_call_target="tpu_custom_call" | custom-call | flops 4294967296 | bytes 9961472 | tf_op jit(solution)/shard_map/pallas_call | solution.py:136
  119.2 1.3 reshape.315.x_ref
  120.6 5.8 %shard_map.126 = f32[32,128]{1,0:T(8,128)} custom-call(f32[32,128]{1,0:T(8,128)} %reshape.315.x_ref), custom_call_target="tpu_custom_call" | custom-call | tf_op jit(solution)/shard_map/pallas_call | solution.py:395
  128.3 1.3 multiply_convert_fusion
  130.5 17.8 %shard_map.127 = bf16[2112,128]{1,0:T(8,128)(2,1)} custom-call(bf16[2112,128]{1,0:T(8,128)(2,1)} %fusion.23.x_ref), custom_call_target="tpu_custom_call" | custom-call | tf_op jit(solution)/shard_map/pallas_call | solution.py:275
  148.3 1.1 slice.74
  150.5 1.2 copy.167
  151.7 8.1 %all-to-all-start = ((bf16[16,272,128]{2,1,0:T(8,128)(2,1)}), bf16[16,272,128]{2,1,0:T(8,128)(2,1)}, u32[]{:S(2)}, u32[]{:S(2)}) async-start(bf16[16,272,128]{2,1,0:T(8,128)(2,1)} %bitcast.30), calls=%async_computation | async-start | bytes 2228224 | tf_op jit(solution)/shard_map/all_to_all | solution.py:536
  159.7 1.5 reshape.342
  161.3 1.1 convert_element_type.91
  166.0 2.4 %fusion.4 = (f32[8,64,2,4]{1,3,2,0:T(4,128)S(1)}, f32[8,2,64,64,4]{3,2,4,1,0:T(8,128)S(1)}) fusion(pred[8,64,64]{1,2,0:T(8,128)(4,1)S(1)} %copy.135, bf16[8,64,2,4,64]{4,3,2,1,0:T(4,128)(2,1)} %reshape.342, bf16[8,64,2,64,1]{1,0,3,2,4:T(8,128)(2,1)S(1)} %bitcast.105), kind=kOutput, calls=%fused_computation.12 | convolution fusion | flops 34336768 | bytes 1753088 | tf_op jit(solution)/shard_map/rtkgd,rukd->rtkgu/dot_general | solution.py:84
  169.1 20.0 %all-to-all-done = bf16[16,272,128]{2,1,0:T(8,128)(2,1)} async-done(((bf16[16,272,128]{2,1,0:T(8,128)(2,1)}), bf16[16,272,128]{2,1,0:T(8,128)(2,1)}, u32[]{:S(2)}, u32[]{:S(2)}) %all-to-all-start) | async-done | bytes 1114144 | tf_op jit(solution)/shard_map/all_to_all | solution.py:536
  189.1 1.6 fusion
  194.8 4.1 %reshape.324 = f32[8,64,4,2,64]{4,3,2,1,0:T(2,128)} reshape(f32[8,32768]{1,0:T(8,128)} %slice.91) | data formatting | bytes 2097152 | tf_op jit(solution)/shard_map/reshape | solution.py:543
  198.9 4.1 %copy.132 = f32[8,64,4,2,64]{1,4,2,3,0:T(8,128)} copy(f32[8,64,4,2,64]{4,3,2,1,0:T(2,128)} %reshape.324) | data formatting | bytes 2097152 | tf_op jit(solution)/shard_map/reshape | solution.py:543
  203.1 2.5 %fusion.3 = bf16[8,64,2,4,64]{1,4,3,2,0:T(8,128)(2,1)S(1)} fusion(f32[8,64,4,2,64]{1,4,2,3,0:T(8,128)} %copy.132, f32[8,2,64,64,4]{3,2,4,1,0:T(8,128)S(1)} %get-tuple-element.42, f32[8,64,2,4]{1,3,2,0:T(4,128)S(1)} %get-tuple-element.22, f32[8,64,2,4]{1,3,2,0:T(4,128)S(1)} %get-tuple-element.23, f32[8,64,2,4]{1,3,2,0:T(4,128)S(1)} %get-tuple-element.41, ...), kind=kOutput, calls=%fused_computation.8 | convolution fusion | flops 36175872 | bytes 2850816 | tf_op jit(solution)/shard_map/rtkgu,rukd->rtkgd/dot_general | solution.py:91
  207.4 1.1 convert_element_type.111.x_ref
  208.5 11.8 %shard_map.128 = f32[512,128]{1,0:T(8,128)} custom-call(bf16[2048,128]{1,0:T(8,128)(2,1)} %convert_element_type.111.x_ref), custom_call_target="tpu_custom_call" | custom-call | tf_op jit(solution)/shard_map/pallas_call | solution.py:275
  221.3 1.7 select_convert_fusion
  (125 shorter events, 26.9 us)
Async XLA Ops:
  0.6 2.1 copy-start
  32.2 1.2 copy-start.8
  32.2 2.0 copy-start.7
  34.2 3.4 %copy-start.11 = (s32[128]{0:T(128)S(1)}, s32[128]{0:T(128)}, u32[]{:S(2)}) copy-start(s32[128]{0:T(128)} %param.17) | copy-start | bytes 1540
  58.4 2.0 copy-start.2
  129.6 19.8 %copy-start.3 = (f32[32,128]{1,0:T(8,128)S(1)}, f32[32,128]{1,0:T(8,128)}, u32[]{:S(2)}) copy-start(f32[32,128]{1,0:T(8,128)} %shard_map.126) | copy-start | bytes 49156
  148.3 1.6 slice-start
  151.7 9.6 %copy-start.1 = (bf16[512,512]{1,0:T(8,128)(2,1)S(1)}, bf16[512,512]{1,0:T(8,128)(2,1)}, u32[]{:S(2)}) copy-start(bf16[512,512]{1,0:T(8,128)(2,1)} %param.11) | copy-start | bytes 1572868
  151.7 37.4 %all-to-all-start = ((bf16[16,272,128]{2,1,0:T(8,128)(2,1)}), bf16[16,272,128]{2,1,0:T(8,128)(2,1)}, u32[]{:S(2)}, u32[]{:S(2)}) async-start(bf16[16,272,128]{2,1,0:T(8,128)(2,1)} %bitcast.30), calls=%async_computation | async-start | bytes 2228224 | tf_op jit(solution)/shard_map/all_to_all | solution.py:536
  161.3 3.0 %copy-start.12 = (s32[8]{0:T(128)S(1)}, s32[8]{0:T(128)}, u32[]{:S(2)}) copy-start(s32[8]{0:T(128)} %param.21) | copy-start | bytes 100
  161.3 3.1 %copy-start.6 = (bf16[8,64,64]{2,1,0:T(8,128)(2,1)S(1)}, bf16[8,64,64]{2,1,0:T(8,128)(2,1)}, u32[]{:S(2)}) copy-start(bf16[8,64,64]{2,1,0:T(8,128)(2,1)} %get-tuple-element.40) | copy-start | bytes 196612
  161.3 4.0 %copy-start.13 = (s32[8]{0:T(128)S(1)}, s32[8]{0:T(128)}, u32[]{:S(2)}) copy-start(s32[8]{0:T(128)} %param.20) | copy-start | bytes 100
  198.9 4.2 %copy-start.4 = (f32[8,2,64,4]{2,3,1,0:T(4,128)S(1)}, f32[8,2,64,4]{2,3,1,0:T(4,128)}, u32[]{:S(2)}) copy-start(f32[8,2,64,4]{2,3,1,0:T(4,128)} %copy.134) | copy-start | bytes 49156
  198.9 4.2 %copy-start.5 = (f32[8,2,64,4]{2,3,1,0:T(4,128)S(1)}, f32[8,2,64,4]{2,3,1,0:T(4,128)}, u32[]{:S(2)}) copy-start(f32[8,2,64,4]{2,3,1,0:T(4,128)} %copy.143) | copy-start | bytes 49156
  205.6 1.3 copy-start.10
  206.9 14.4 %copy-start.9 = (pred[128]{0:T(512)(128)(4,1)S(1)}, pred[128]{0:T(512)(128)(4,1)}, u32[]{:S(2)}) copy-start(pred[128]{0:T(512)(128)(4,1)} %fusion.59) | copy-start | bytes 388
